TPU v7x, 256 devices: a whole 4x4x8 slice. The times are simulated.
256 devices in a mesh: row: 8 (over z_hi, y), col: 4 (over x), band: 8 (over z_lo, core).
Axes of the slice: x: 4, y: 4, z: 8 (z_hi: 2, z_lo: 4; z = z_hi * 4 + z_lo), core: 2. Of those that a mesh axis runs over, the one named last changes fastest.
Arguments:
- vis: bfloat16 [64, 4, 2, 512, 512], P('band', None, None, 'row', 'col'), may hold values from -200 to 200
- flags: int32 [64, 4, 512], P('band'), may hold values 0 or 1
- positions: float32 [4, 3, 512], replicated, may hold values from -4 to 4
- lmn: float32 [3, 8], replicated, may hold values from -3 to 3
- flux: float32 [64, 8], P('band'), may hold values from 0.5 to 2
- gains: float32 [64, 4, 2, 8, 512], P('band', None, None, None, ('row', 'col')), may hold values from -6 to 6
- duals: float32 [64, 4, 2, 8, 512], P('band', None, None, None, ('row', 'col')), may hold values from -2 to 2
Outputs:
- gains_out: float32 [64, 4, 2, 8, 512], P('band', None, None, None, ('row', 'col'))
- duals_out: float32 [64, 4, 2, 8, 512], P('band', None, None, None, ('row', 'col'))
All inputs are finite; a program needn't handle non-finite values. No bound on the sum of `flags` on one device may be relied on, other than what follows from the above.
Results may differ from a plain program's by a relative error of at most 0.0003.
Values sent between devices are 32-bit elements; how exact they have to be, the bound alone decides.
A program may use at most 128 MiB of HBM per device.

v0:
```python
import functools
import math

import jax
import jax.numpy as jnp
from jax import lax
from jax.sharding import Mesh
from jax.sharding import PartitionSpec as P

S = 512
F = 64
ITERS = 2
BAND = ("band_0", "band_1")
ROW = ("row_0", "row_1")
ROW_COL_BAND = ("row_0", "row_1", "col", "band_0", "band_1")
ROW_COL = ("row_0", "row_1", "col")


PENALTY = 0.05
HIGH = lax.Precision.HIGHEST


def sent_to_all(array, axis):
    length = lax.axis_size(axis)
    return lax.all_to_all(
        jnp.broadcast_to(array[None], (length, *array.shape)), axis, 0, 0, tiled=True
    )


def taken_together(array, axis):
    return sent_to_all(array, axis).sum(axis=0)


def joined_along(pieces, dim):
    pieces = jnp.moveaxis(pieces, 0, dim)
    dims = pieces.shape
    return pieces.reshape(*dims[:dim], dims[dim] * dims[dim + 1], *dims[dim + 2 :])


def gathered_copies(array, axis, dim):
    pieces = sent_to_all(array, axis)
    return joined_along(pieces, dim)


def one_axis_at_a_time(array, axes):
    return functools.reduce(lax.psum, axes, array)


def split_up(array, dim, length):
    dims = array.shape
    pieces = array.reshape(*dims[:dim], length, dims[dim] // length, *dims[dim + 1 :])
    return jnp.moveaxis(pieces, dim, 0)


def sum_at_owner(array, axis, dim):
    length = lax.axis_size(axis)
    pieces = lax.all_to_all(split_up(array, dim, length), axis, 0, 0, tiled=True)
    return jnp.sum(pieces, axis=0)


def basis(count):
    grid = 2.0 * jnp.arange(count, dtype=jnp.float32) / (count - 1) - 1.0
    return jnp.stack([grid**power for power in range(4)], axis=1)


def rotate(positions, lmn, freq):
    geometry = jnp.einsum("tks,kd->tds", positions, lmn, precision=HIGH)
    angle = 2.0 * math.pi * freq[:, None, None, None] * geometry[None]
    return (jnp.cos(angle), -jnp.sin(angle))


def complex_mul(a_re, a_im, b_re, b_im):
    return (a_re * b_re - a_im * b_im, a_re * b_im + a_im * b_re)


def solve_fit(rhs):
    full = basis(F)
    gram = jnp.dot(full.T, full, precision=HIGH)
    factor = jnp.linalg.cholesky(gram)
    flat = rhs.reshape(rhs.shape[0], -1)
    return jax.scipy.linalg.cho_solve((factor, True), flat).reshape(rhs.shape)


def shards(vis, flags, positions, lmn, flux, gains, duals):
    width = gains.shape[0]
    first = lax.axis_index(BAND) * width
    local_basis = lax.dynamic_slice_in_dim(basis(F), first, width, 0)
    freq = 1.0 + (first + jnp.arange(width, dtype=jnp.int32)).astype(jnp.float32) / F
    row_index = lax.axis_index(ROW)
    col_index = lax.axis_index("col")
    row_count = vis.shape[3]
    col_count = vis.shape[4]
    owned = gains.shape[4]
    own_start = (row_index * lax.axis_size("col") + col_index) * owned
    row_start = row_index * row_count
    col_start = col_index * col_count
    own_cos, own_sin = rotate(lax.dynamic_slice_in_dim(positions, own_start, owned, 2), lmn, freq)
    row_cos, row_sin = rotate(
        lax.dynamic_slice_in_dim(positions, row_start, row_count, 2), lmn, freq
    )
    col_cos, col_sin = rotate(
        lax.dynamic_slice_in_dim(positions, col_start, col_count, 2), lmn, freq
    )
    all_live = flags.astype(jnp.float32)
    row_live = lax.dynamic_slice_in_dim(all_live, row_start, row_count, 2)
    col_live = lax.dynamic_slice_in_dim(all_live, col_start, col_count, 2)
    row_ids = row_start + jnp.arange(row_count, dtype=jnp.int32)
    col_ids = col_start + jnp.arange(col_count, dtype=jnp.int32)
    distinct = (row_ids[:, None] != col_ids[None, :]).astype(jnp.float32)
    weight = row_live[:, :, :, None] * col_live[:, :, None, :] * distinct
    vis_re = vis[:, :, 0].astype(jnp.float32)
    vis_im = vis[:, :, 1].astype(jnp.float32)
    scale = flux[:, None, :, None]

    def fit(gain, dual):
        rhs = jnp.einsum("fk,ftcds->ktcds", local_basis, gain + dual, precision=HIGH)
        return solve_fit(taken_together(rhs, BAND))

    gain, dual = (gains, duals)
    coeffs = fit(gain, dual)
    for step in range(ITERS):
        target = jnp.einsum("fk,ktcds->ftcds", local_basis, coeffs, precision=HIGH) - dual
        row_gain = gathered_copies(gain, "col", 4)
        every = gathered_copies(row_gain, ROW, 4)
        col_gain = lax.dynamic_slice_in_dim(every, col_start, col_count, 4)
        row_re, row_im = complex_mul(row_gain[:, :, 0], row_gain[:, :, 1], row_cos, row_sin)
        col_re, col_im = complex_mul(col_gain[:, :, 0], col_gain[:, :, 1], col_cos, col_sin)
        col_re = scale * col_re
        col_im = scale * col_im
        model_re = jnp.einsum("ftdp,ftdq->ftpq", row_re, col_re, precision=HIGH) + jnp.einsum(
            "ftdp,ftdq->ftpq", row_im, col_im, precision=HIGH
        )
        model_im = jnp.einsum("ftdp,ftdq->ftpq", row_im, col_re, precision=HIGH) - jnp.einsum(
            "ftdp,ftdq->ftpq", row_re, col_im, precision=HIGH
        )
        resid_re = weight * (vis_re - model_re)
        resid_im = weight * (vis_im - model_im)
        squares, samples = (
            one_axis_at_a_time(jnp.sum(resid_re * resid_re + resid_im * resid_im), ROW_COL_BAND),
            one_axis_at_a_time(jnp.sum(weight), ROW_COL_BAND),
        )
        sum_re = jnp.einsum("ftpq,ftdq->ftdp", resid_re, col_re, precision=HIGH) - jnp.einsum(
            "ftpq,ftdq->ftdp", resid_im, col_im, precision=HIGH
        )
        sum_im = jnp.einsum("ftpq,ftdq->ftdp", resid_re, col_im, precision=HIGH) + jnp.einsum(
            "ftpq,ftdq->ftdp", resid_im, col_re, precision=HIGH
        )
        denom = jnp.einsum(
            "ftpq,ftdq->ftdp", weight, col_re * col_re + col_im * col_im, precision=HIGH
        )
        terms = jnp.stack([sum_re, sum_im, denom], axis=2)
        shares = sum_at_owner(terms, "col", 4)
        pairs = shares[:, :, 0:2]
        own_denom = shares[:, :, 2:3]
        num_re, num_im = complex_mul(own_cos, -own_sin, pairs[:, :, 0], pairs[:, :, 1])
        numer = jnp.stack([num_re, num_im], axis=2)
        rho = PENALTY * S * (squares / samples + 1e-06)
        fresh = (numer + own_denom * gain + rho * target) / (own_denom + rho)
        gain = 0.5 * (gain + fresh)
        coeffs = fit(gain, dual)
        dual = dual + gain - jnp.einsum("fk,ktcds->ftcds", local_basis, coeffs, precision=HIGH)
    return (gain, dual)


def solution(mesh):
    finer = Mesh(
        mesh.devices.reshape(2, 4, mesh.shape["col"], 4, 2),
        ("row_0", "row_1", "col", "band_0", "band_1"),
    )
    return jax.shard_map(
        shards,
        mesh=finer,
        in_specs=(
            P(BAND, None, None, ROW, "col"),
            P(BAND, None, None),
            P(),
            P(),
            P(BAND, None),
            P(BAND, None, None, None, ROW_COL),
            P(BAND, None, None, None, ROW_COL),
        ),
        out_specs=(P(BAND, None, None, None, ROW_COL), P(BAND, None, None, None, ROW_COL)),
        check_vma=False,
    )
```

profile of v0, /device:TPU:1, one launch (start us, length us, event | category | flops | bytes accessed | tf_op | source)
XLA Modules:
  0.0 315.6 jit_solution(6262773476866017170)
XLA Ops:
  2.8 4.8 %all-to-all-start = ((f32[4,1,8192]{2,1,0:T(1,128)}), f32[4,1,8192]{2,1,0:T(1,128)S(1)}, u32[]{:S(2)}, u32[]{:S(2)}) async-start(f32[4,1,8192]{2,1,0:T(1,128)} %reshape.163), calls=%async_computation | async-start | bytes 262144 | tf_op jit(solution)/shard_map/all_to_all | solution.py:25
  12.5 8.0 %all-to-all-start.3 = ((f32[8,1,4096]{2,1,0:T(1,128)}), f32[8,1,4096]{2,1,0:T(1,128)}, u32[]{:S(2)}, u32[]{:S(2)}) async-start(f32[8,1,4096]{2,1,0:T(1,128)} %reshape.169), calls=%async_computation.3 | async-start | bytes 262144 | tf_op jit(solution)/shard_map/all_to_all | solution.py:25
  26.4 9.1 %all-to-all-start.1 = ((f32[8,1,32768]{2,1,0:T(1,128)}), f32[8,1,32768]{2,1,0:T(1,128)S(1)}, u32[]{:S(2)}, u32[]{:S(2)}) async-start(f32[8,1,32768]{2,1,0:T(1,128)} %reshape.165), calls=%async_computation.1 | async-start | bytes 2097152 | tf_op jit(solution)/shard_map/all_to_all | solution.py:25
  41.1 10.6 %all-to-all-done.1 = f32[8,1,32768]{2,1,0:T(1,128)S(1)} async-done(((f32[8,1,32768]{2,1,0:T(1,128)}), f32[8,1,32768]{2,1,0:T(1,128)S(1)}, u32[]{:S(2)}, u32[]{:S(2)}) %all-to-all-start.1) | async-done | bytes 1048608 | tf_op jit(solution)/shard_map/all_to_all | solution.py:25
  74.8 4.6 %add_reduce_fusion.1 = (f32[]{:T(128)}, f32[8,4,64,128]{3,2,1,0:T(8,128)S(1)}) fusion(f32[8,4,64,128]{3,2,1,0:T(8,128)S(1)} %fusion.1, f32[8,4,64,128]{3,2,1,0:T(8,128)} %fusion.117, f32[8,4,8,128]{3,2,1,0:T(8,128)} %copy-done.7, f32[8,4,2,8,64]{4,3,2,1,0:T(8,128)S(1)} %broadcast_in_dim.19, f32[4,8,64]{2,1,0:T(8,128)S(1)} %convolution_bitcast_fusion, ...), kind=kOutput, calls=%fused_computation.28 | convolution fusion | flops 27869184 | bytes 3997732 | tf_op jit(solution)/shard_map/ftdp,ftdq->ftpq/dot_general | solution.py:133
  87.7 3.4 %all-to-all-start.2 = ((f32[4,1,12288]{2,1,0:T(1,128)}), f32[4,1,12288]{2,1,0:T(1,128)S(1)}, u32[]{:S(2)}, u32[]{:S(2)}) async-start(f32[4,1,12288]{2,1,0:T(1,128)} %reshape.167), calls=%async_computation.2 | async-start | bytes 393216 | tf_op jit(solution)/shard_map/all_to_all | solution.py:57
  92.0 8.4 %all-reduce.4 = (f32[]{:T(128)}, f32[]{:T(128)}) all-reduce(f32[]{:T(128)} %get-tuple-element.40, f32[]{:T(128)} %fusion.13), channel_id=1, replica_groups=mesh['row_0'=2,'row_1'=4,'col'=4,'band_0'=4,'band_1'=2] {'row_0'}, use_global_device_ids=true, to_apply=%region_2.3 | all-reduce | flops 2 | bytes 16 | tf_op jit(solution)/shard_map/psum | solution.py:46
  100.4 9.5 %all-reduce.2 = (f32[]{:T(128)}, f32[]{:T(128)}) all-reduce(f32[]{:T(128)} %get-tuple-element.20, f32[]{:T(128)} %get-tuple-element.21), channel_id=1, replica_groups=mesh['row_0'=2,'row_1'=4,'col'=4,'band_0'=4,'band_1'=2] {'row_1'}, use_global_device_ids=true, to_apply=%region_3.4 | all-reduce | flops 2 | bytes 16 | tf_op jit(solution)/shard_map/psum | solution.py:46
  109.9 9.1 %all-reduce.1 = (f32[]{:T(128)}, f32[]{:T(128)}) all-reduce(f32[]{:T(128)} %get-tuple-element.16, f32[]{:T(128)} %get-tuple-element.17), channel_id=1, replica_groups=mesh['row_0'=2,'row_1'=4,'col'=4,'band_0'=4,'band_1'=2] {'col'}, use_global_device_ids=true, to_apply=%region_4.5 | all-reduce | flops 2 | bytes 16 | tf_op jit(solution)/shard_map/psum | solution.py:46
  119.0 19.6 %all-reduce = (f32[]{:T(128)}, f32[]{:T(128)}) all-reduce(f32[]{:T(128)} %get-tuple-element.14, f32[]{:T(128)} %get-tuple-element.15), channel_id=1, replica_groups=mesh['row_0'=2,'row_1'=4,'col'=4,'band_0'=4,'band_1'=2] {'band_0'}, use_global_device_ids=true, to_apply=%region_5.6 | all-reduce | flops 2 | bytes 16 | tf_op jit(solution)/shard_map/psum | solution.py:46
  138.6 12.0 %all-reduce.3 = (f32[]{:T(128)}, f32[]{:T(128)}) all-reduce(f32[]{:T(128)} %get-tuple-element.12, f32[]{:T(128)} %get-tuple-element.13), channel_id=1, replica_groups=mesh['row_0'=2,'row_1'=4,'col'=4,'band_0'=4,'band_1'=2] {'band_1'}, use_global_device_ids=true, to_apply=%region_6.7 | all-reduce | flops 2 | bytes 16 | tf_op jit(solution)/shard_map/psum | solution.py:46
  164.8 5.3 %all-to-all-start.7 = ((f32[8,1,4096]{2,1,0:T(1,128)}), f32[8,1,4096]{2,1,0:T(1,128)}, u32[]{:S(2)}, u32[]{:S(2)}) async-start(f32[8,1,4096]{2,1,0:T(1,128)} %reshape.177), calls=%async_computation.7 | async-start | bytes 262144 | tf_op jit(solution)/shard_map/all_to_all | solution.py:25
  176.1 3.8 %all-to-all-start.5 = ((f32[8,1,32768]{2,1,0:T(1,128)}), f32[8,1,32768]{2,1,0:T(1,128)S(1)}, u32[]{:S(2)}, u32[]{:S(2)}) async-start(f32[8,1,32768]{2,1,0:T(1,128)} %reshape.173), calls=%async_computation.5 | async-start | bytes 2097152 | tf_op jit(solution)/shard_map/all_to_all | solution.py:25
  186.2 11.7 %all-to-all-done.5 = f32[8,1,32768]{2,1,0:T(1,128)S(1)} async-done(((f32[8,1,32768]{2,1,0:T(1,128)}), f32[8,1,32768]{2,1,0:T(1,128)S(1)}, u32[]{:S(2)}, u32[]{:S(2)}) %all-to-all-start.5) | async-done | bytes 1048608 | tf_op jit(solution)/shard_map/all_to_all | solution.py:25
  197.9 4.5 %reduce.9 = f32[8,32768]{1,0:T(8,128)} reduce(f32[8,1,32768]{2,1,0:T(1,128)S(1)} %all-to-all-done.5, f32[]{:T(128)} %broadcast.222), dimensions={1}, to_apply=%all_to_all.32.reduce_sub_computation | reduce | bytes 2097156 | tf_op jit(solution)/shard_map/all_to_all | solution.py:25
  211.7 3.7 %fusion.111 = f32[8,4,64,128]{3,2,1,0:T(8,128)} fusion(f32[8,4,8,128]{3,2,1,0:T(8,128)S(1)} %get-tuple-element.24, f32[8,4,2,8,64]{4,3,1,0,2:T(8,128)S(1)} %reshape.161, f32[4,8,64]{2,1,0:T(8,128)S(1)} %convolution_bitcast_fusion, f32[8]{0:T(128)S(1)} %add_multiply_fusion), kind=kOutput, calls=%fused_computation.164 | convolution fusion | flops 25247744 | bytes 1318944 | tf_op jit(solution)/shard_map/ftdp,ftdq->ftpq/dot_general | solution.py:133
  225.6 4.6 %add_reduce_fusion = (f32[]{:T(128)}, f32[8,4,64,128]{3,2,1,0:T(8,128)S(1)}) fusion(f32[8,4,64,128]{3,2,1,0:T(8,128)S(1)} %fusion.5, f32[8,4,64,128]{3,2,1,0:T(8,128)} %fusion.111, f32[8,4,8,128]{3,2,1,0:T(8,128)} %copy-done.3, f32[8,4,2,8,64]{4,3,1,0,2:T(8,128)S(1)} %reshape.161, f32[4,8,64]{2,1,0:T(8,128)S(1)} %convolution_bitcast_fusion, ...), kind=kOutput, calls=%fused_computation.27 | convolution fusion | flops 27869184 | bytes 3997732 | tf_op jit(solution)/shard_map/ftdp,ftdq->ftpq/dot_general | solution.py:133
  235.3 8.2 %psum.130 = f32[]{:T(128)} all-reduce(f32[]{:T(128)} %get-tuple-element.44), channel_id=1, replica_groups=mesh['row_0'=2,'row_1'=4,'col'=4,'band_0'=4,'band_1'=2] {'row_0'}, use_global_device_ids=true, to_apply=%region_18.0 | all-reduce | flops 1 | bytes 8 | tf_op jit(solution)/shard_map/psum | solution.py:46
  245.0 9.7 %psum.131 = f32[]{:T(128)} all-reduce(f32[]{:T(128)} %psum.130), channel_id=1, replica_groups=mesh['row_0'=2,'row_1'=4,'col'=4,'band_0'=4,'band_1'=2] {'row_1'}, use_global_device_ids=true, to_apply=%region_19.0 | all-reduce | flops 1 | bytes 8 | tf_op jit(solution)/shard_map/psum | solution.py:46
  258.0 9.3 %psum.132 = f32[]{:T(128)} all-reduce(f32[]{:T(128)} %psum.131), channel_id=1, replica_groups=mesh['row_0'=2,'row_1'=4,'col'=4,'band_0'=4,'band_1'=2] {'col'}, use_global_device_ids=true, to_apply=%region_20.0 | all-reduce | flops 1 | bytes 8 | tf_op jit(solution)/shard_map/psum | solution.py:46
  267.5 16.8 %psum.133 = f32[]{:T(128)} all-reduce(f32[]{:T(128)} %psum.132), channel_id=1, replica_groups=mesh['row_0'=2,'row_1'=4,'col'=4,'band_0'=4,'band_1'=2] {'band_0'}, use_global_device_ids=true, to_apply=%region_21.0 | all-reduce | flops 1 | bytes 8 | tf_op jit(solution)/shard_map/psum | solution.py:46
  284.4 11.9 %psum.134 = f32[]{:T(128)} all-reduce(f32[]{:T(128)} %psum.133), channel_id=1, replica_groups=mesh['row_0'=2,'row_1'=4,'col'=4,'band_0'=4,'band_1'=2] {'band_1'}, use_global_device_ids=true, to_apply=%region_22.0 | all-reduce | flops 1 | bytes 8 | tf_op jit(solution)/shard_map/psum | solution.py:46
  302.7 3.6 %all-to-all-start.8 = ((f32[8,1,4096]{2,1,0:T(1,128)}), f32[8,1,4096]{2,1,0:T(1,128)S(1)}, u32[]{:S(2)}, u32[]{:S(2)}) async-start(f32[8,1,4096]{2,1,0:T(1,128)} %reshape.179), calls=%async_computation.8 | async-start | bytes 262144 | tf_op jit(solution)/shard_map/all_to_all | solution.py:25
  307.0 5.1 %all-to-all-done.8 = f32[8,1,4096]{2,1,0:T(1,128)S(1)} async-done(((f32[8,1,4096]{2,1,0:T(1,128)}), f32[8,1,4096]{2,1,0:T(1,128)S(1)}, u32[]{:S(2)}, u32[]{:S(2)}) %all-to-all-start.8) | async-done | bytes 131104 | tf_op jit(solution)/shard_map/all_to_all | solution.py:25
  (211 shorter events, 114.2 us)
Async XLA Ops:
  0.6 35.2 %copy-start = (f32[4,3,512]{2,0,1:T(4,128)S(1)}, f32[4,3,512]{2,0,1:T(4,128)}, u32[]{:S(2)}) copy-start(f32[4,3,512]{2,0,1:T(4,128)} %param.12) | copy-start | bytes 73732
  0.6 7.1 %copy-start.11 = (f32[8,4,2,8,16]{4,3,2,1,0:T(8,128)S(1)}, f32[8,4,2,8,16]{4,3,2,1,0:T(8,128)}, u32[]{:S(2)}) copy-start(f32[8,4,2,8,16]{4,3,2,1,0:T(8,128)} %param.15) | copy-start | bytes 98308
  0.7 7.1 %copy-start.13 = (f32[8,4,2,8,16]{4,3,2,1,0:T(8,128)S(1)}, f32[8,4,2,8,16]{4,3,2,1,0:T(8,128)}, u32[]{:S(2)}) copy-start(f32[8,4,2,8,16]{4,3,2,1,0:T(8,128)} %param.16) | copy-start | bytes 98308
  2.8 9.7 %all-to-all-start = ((f32[4,1,8192]{2,1,0:T(1,128)}), f32[4,1,8192]{2,1,0:T(1,128)S(1)}, u32[]{:S(2)}, u32[]{:S(2)}) async-start(f32[4,1,8192]{2,1,0:T(1,128)} %reshape.163), calls=%async_computation | async-start | bytes 262144 | tf_op jit(solution)/shard_map/all_to_all | solution.py:25
  12.5 13.9 %all-to-all-start.3 = ((f32[8,1,4096]{2,1,0:T(1,128)}), f32[8,1,4096]{2,1,0:T(1,128)}, u32[]{:S(2)}, u32[]{:S(2)}) async-start(f32[8,1,4096]{2,1,0:T(1,128)} %reshape.169), calls=%async_computation.3 | async-start | bytes 262144 | tf_op jit(solution)/shard_map/all_to_all | solution.py:25
  25.9 9.6 %copy-start.26 = (s32[8,4,512]{2,1,0:T(4,128)S(1)}, s32[8,4,512]{2,1,0:T(4,128)}, u32[]{:S(2)}) copy-start(s32[8,4,512]{2,1,0:T(4,128)} %param.11) | copy-start | bytes 196612
  25.9 11.3 %copy-start.30 = (f32[3,8]{1,0:T(4,128)S(1)}, f32[3,8]{1,0:T(4,128)}, u32[]{:S(2)}) copy-start(f32[3,8]{1,0:T(4,128)} %param.13) | copy-start | bytes 292
  26.4 25.3 %all-to-all-start.1 = ((f32[8,1,32768]{2,1,0:T(1,128)}), f32[8,1,32768]{2,1,0:T(1,128)S(1)}, u32[]{:S(2)}, u32[]{:S(2)}) async-start(f32[8,1,32768]{2,1,0:T(1,128)} %reshape.165), calls=%async_computation.1 | async-start | bytes 2097152 | tf_op jit(solution)/shard_map/all_to_all | solution.py:25
  58.4 10.4 %copy-start.7 = (f32[8,4,8,128]{3,2,1,0:T(8,128)}, f32[8,4,8,128]{3,2,1,0:T(8,128)S(1)}, u32[]{:S(2)}) copy-start(f32[8,4,8,128]{3,2,1,0:T(8,128)S(1)} %get-tuple-element.27) | copy-start | bytes 393220
  58.4 12.8 %copy-start.9 = (f32[8,4,8,128]{3,2,1,0:T(8,128)}, f32[8,4,8,128]{3,2,1,0:T(8,128)S(1)}, u32[]{:S(2)}) copy-start(f32[8,4,8,128]{3,2,1,0:T(8,128)S(1)} %get-tuple-element.26) | copy-start | bytes 393220
  60.7 5.6 %copy-start.2 = (bf16[8,4,2,64,128]{4,3,2,1,0:T(8,128)(2,1)S(1)}, bf16[8,4,2,64,128]{4,3,2,1,0:T(8,128)(2,1)}, u32[]{:S(2)}) copy-start(bf16[8,4,2,64,128]{4,3,2,1,0:T(8,128)(2,1)} %param.10) | copy-start | bytes 3145732
  86.3 4.8 %copy-start.28 = (f32[4,1024]{1,0:T(4,128)S(1)}, f32[4,1024]{1,0:T(4,128)}, u32[]{:S(2)}) copy-start(f32[4,1024]{1,0:T(4,128)} %fusion.93) | copy-start | bytes 49156
  87.7 64.1 %all-to-all-start.2 = ((f32[4,1,12288]{2,1,0:T(1,128)}), f32[4,1,12288]{2,1,0:T(1,128)S(1)}, u32[]{:S(2)}, u32[]{:S(2)}) async-start(f32[4,1,12288]{2,1,0:T(1,128)} %reshape.167), calls=%async_computation.2 | async-start | bytes 393216 | tf_op jit(solution)/shard_map/all_to_all | solution.py:57
  155.4 4.6 %copy-start.19 = (f32[8,4,2,8,16]{4,0,3,2,1:T(8,128)}, f32[8,4,2,8,16]{4,0,3,2,1:T(8,128)S(1)}, u32[]{:S(2)}) copy-start(f32[8,4,2,8,16]{4,0,3,2,1:T(8,128)S(1)} %get-tuple-element.43) | copy-start | bytes 98308
  156.7 8.1 %all-to-all-start.4 = ((f32[4,1,8192]{2,1,0:T(1,128)}), f32[4,1,8192]{2,1,0:T(1,128)S(1)}, u32[]{:S(2)}, u32[]{:S(2)}) async-start(f32[4,1,8192]{2,1,0:T(1,128)} %reshape.171), calls=%async_computation.4 | async-start | bytes 262144 | tf_op jit(solution)/shard_map/all_to_all | solution.py:25
  164.8 11.3 %all-to-all-start.7 = ((f32[8,1,4096]{2,1,0:T(1,128)}), f32[8,1,4096]{2,1,0:T(1,128)}, u32[]{:S(2)}, u32[]{:S(2)}) async-start(f32[8,1,4096]{2,1,0:T(1,128)} %reshape.177), calls=%async_computation.7 | async-start | bytes 262144 | tf_op jit(solution)/shard_map/all_to_all | solution.py:25
  176.1 21.9 %all-to-all-start.5 = ((f32[8,1,32768]{2,1,0:T(1,128)}), f32[8,1,32768]{2,1,0:T(1,128)S(1)}, u32[]{:S(2)}, u32[]{:S(2)}) async-start(f32[8,1,32768]{2,1,0:T(1,128)} %reshape.173), calls=%async_computation.5 | async-start | bytes 2097152 | tf_op jit(solution)/shard_map/all_to_all | solution.py:25
  209.4 10.2 %copy-start.3 = (f32[8,4,8,128]{3,2,1,0:T(8,128)}, f32[8,4,8,128]{3,2,1,0:T(8,128)S(1)}, u32[]{:S(2)}) copy-start(f32[8,4,8,128]{3,2,1,0:T(8,128)S(1)} %get-tuple-element.25) | copy-start | bytes 393220
  209.4 12.6 %copy-start.5 = (f32[8,4,8,128]{3,2,1,0:T(8,128)}, f32[8,4,8,128]{3,2,1,0:T(8,128)S(1)}, u32[]{:S(2)}) copy-start(f32[8,4,8,128]{3,2,1,0:T(8,128)S(1)} %get-tuple-element.24) | copy-start | bytes 393220
  233.1 10.5 %copy-start.16 = (f32[8,4,1,8,4,16]{5,3,1,0,2,4:T(8,128)S(1)}, f32[8,4,1,8,4,16]{5,3,1,0,2,4:T(8,128)}, u32[]{:S(2)}) copy-start(f32[8,4,1,8,4,16]{5,3,1,0,2,4:T(8,128)} %copy.160) | copy-start | bytes 196612
  234.8 8.8 %copy-start.18 = (f32[8,4,1,8,4,16]{5,3,1,0,2,4:T(8,128)S(1)}, f32[8,4,1,8,4,16]{5,3,1,0,2,4:T(8,128)}, u32[]{:S(2)}) copy-start(f32[8,4,1,8,4,16]{5,3,1,0,2,4:T(8,128)} %copy.159) | copy-start | bytes 196612
  243.7 23.6 %copy-start.27 = (f32[4,1024]{1,0:T(4,128)S(1)}, f32[4,1024]{1,0:T(4,128)}, u32[]{:S(2)}) copy-start(f32[4,1024]{1,0:T(4,128)} %fusion.89) | copy-start | bytes 49156
  254.7 42.9 %all-to-all-start.6 = ((f32[4,1,12288]{2,1,0:T(1,128)}), f32[4,1,12288]{2,1,0:T(1,128)S(1)}, u32[]{:S(2)}, u32[]{:S(2)}) async-start(f32[4,1,12288]{2,1,0:T(1,128)} %reshape.175), calls=%async_computation.6 | async-start | bytes 393216 | tf_op jit(solution)/shard_map/all_to_all | solution.py:57
  302.7 9.5 %all-to-all-start.8 = ((f32[8,1,4096]{2,1,0:T(1,128)}), f32[8,1,4096]{2,1,0:T(1,128)S(1)}, u32[]{:S(2)}, u32[]{:S(2)}) async-start(f32[8,1,4096]{2,1,0:T(1,128)} %reshape.179), calls=%async_computation.8 | async-start | bytes 262144 | tf_op jit(solution)/shard_map/all_to_all | solution.py:25
  (16 other events, 39.4 us)
where the time goes:
time: 321 us; the launch traced here: 316 us
  blocking collectives  114 us (36%)
  matrix products  52.7 us (16%)
  starting transfers between devices  44.7 us (14%)
  local copies, waits for them, and re-layouts  39.9 us (12%)
  waiting for transfers between devices  32.7 us (10%)
  other arithmetic  26.9 us (8%)
  between operations  4.21 us (1%)
    psum x10, blocking collectives, one_axis_at_a_time(): return functools.reduce(lax.psum, axes, array)  114 us
    all_to_all x7, starting transfers between devices, sent_to_all(): lax.all_to_all(jnp.broadcast_to(array[None], (length, *array.shape)), axi...  38 us
    all_to_all x7, waiting for transfers between devices, sent_to_all(): lax.all_to_all(jnp.broadcast_to(array[None], (length, *array.shape)), axi...  32.7 us
    unnamed x86, local copies, waits for them, and re-layouts  22.9 us
    all_to_all x7, other arithmetic, sent_to_all(): lax.all_to_all(jnp.broadcast_to(array[None], (length, *array.shape)), axi...  15 us
    dot_general x2, matrix products, shards(): jnp.einsum('ftdp,ftdq->ftpq', row_re, col_im, precision=HIGH)  9.12 us
    dot_general x2, matrix products, shards(): jnp.einsum('ftdp,ftdq->ftpq', row_im, col_re, precision=HIGH)  6.91 us
    all_to_all x2, starting transfers between devices, sum_at_owner(): lax.all_to_all(split_up(array, dim, length), axis, 0, 0, tiled=True)  6.73 us
  transfers between devices with their start and end apart: 9, of which 7 were waited for; matrix products, arithmetic and copies ran while one was open for 9% of the time, Pallas kernels for 0%

commit v1 on v0

v1 whole, which is shorter than its diff:
```python
import functools
import math

import jax
import jax.numpy as jnp
import numpy as np
from jax import lax
from jax.experimental import pallas as pl
from jax.experimental.pallas import tpu as pltpu
from jax.sharding import Mesh
from jax.sharding import PartitionSpec as P

S = 512
F = 64
ITERS = 2
PENALTY = 0.05
AXES = ("zh", "y", "x", "zl", "core")
BAND = ("zl", "core")
ROW = ("zh", "y")
OWN = ("zh", "y", "x")
MESH = pl.DeviceIdType.MESH
HIGH = lax.Precision.HIGHEST
F32 = jnp.float32
BF16 = jnp.bfloat16
PAIRS = 4
OWNED = 16
LANES = 128


def fit_polynomials():
    grid = 2.0 * np.arange(F, dtype=np.float64) / (F - 1) - 1.0
    powers = np.stack([grid**k for k in range(4)], axis=1)
    _, upper = np.linalg.qr(powers)
    return np.linalg.inv(upper)


def split(value):
    high = value.astype(BF16)
    return high, (value - high.astype(F32)).astype(BF16)


def kernel(
    vis_hbm, flags_ref, pos_ref, lmn_ref, flux_ref, gains_ref, duals_ref,
    gains_out, duals_out,
    vis_buf, wvis, weight, rmat, lhs, rhi,
    row_buf, col_buf, relay_buf, send_buf, num_buf, num_recv,
    t_buf, t_recv, fit_send, fit_recv, sq_send, sq_recv,
    flag_col, flag_row, geom_blk, flux_tab,
    vis_sem, row_s, row_r, rel_s, rel_r, own_s, fwd_s, col_r,
    num_s, num_r, t_s, t_r, sq_s, sq_r, fit_s, fit_r,
):
    me = {axis: lax.axis_index(axis) for axis in AXES}
    zh, y, x = me["zh"], me["y"], me["x"]

    def at(**moved):
        place = dict(me)
        place.update(moved)
        return tuple(place[axis] for axis in AXES)

    x_peers = [at(x=lax.rem(x + k, 4)) for k in range(1, 4)]
    plane_peers = [
        at(y=lax.rem(y + k // 4, 4), x=lax.rem(x + k % 4, 4)) for k in range(1, 16)
    ]
    line_peers = [
        at(
            zh=lax.rem(zh + k // 8, 2),
            zl=lax.rem(me["zl"] + (k // 2) % 4, 4),
            core=lax.rem(me["core"] + k % 2, 2),
        )
        for k in range(1, 16)
    ]
    band_peers = line_peers[:7]

    def push(src, dst, send_sem, recv_sem, device):
        return pltpu.make_async_remote_copy(
            src_ref=src, dst_ref=dst, send_sem=send_sem, recv_sem=recv_sem,
            device_id=device, device_id_type=MESH,
        )

    pending = []

    barrier = pltpu.get_barrier_semaphore()
    for peer in plane_peers + line_peers:
        pl.semaphore_signal(barrier, inc=1, device_id=peer, device_id_type=MESH)
    vis_copy = pltpu.make_async_copy(vis_hbm, vis_buf, vis_sem)
    vis_copy.start()

    lane = lax.broadcasted_iota(jnp.int32, (1, LANES), 1)
    half = lane // 64
    low = lane < 64
    is_im = (lane // 8) % 2 == 1
    sign = jnp.where(is_im, -1.0, 1.0).astype(F32)

    def swapped(value):
        return jnp.where(is_im, pltpu.roll(value, 8, 1), pltpu.roll(value, 120, 1))

    def both(value):
        return value + pltpu.roll(value, 64, 1)

    band = me["zl"] * 2 + me["core"]
    row = zh * 4 + y
    row_block = lax.div(row, 2)
    row_half = pl.multiple_of(lax.rem(row, 2) * 64, 64)
    own_at = pl.multiple_of(lax.rem(row, 2) * 64 + x * OWNED, OWNED)

    dir_hot = (
        lax.broadcasted_iota(jnp.int32, (8, LANES), 0)
        == lax.broadcasted_iota(jnp.int32, (8, LANES), 1) % 8
    ).astype(F32)
    flux_all = jnp.dot(flux_ref[...], dir_hot, precision=HIGH, preferred_element_type=F32)
    for fp in range(PAIRS):
        flux_tab[pl.ds(fp, 1), :] = jnp.where(
            low, flux_all[2 * fp : 2 * fp + 1], flux_all[2 * fp + 1 : 2 * fp + 2]
        )
    lmn_lanes = jnp.dot(lmn_ref[...], dir_hot, precision=HIGH, preferred_element_type=F32)
    time_of = (lane // 16) % 4
    block = pl.ds(pl.multiple_of(row_block * LANES, LANES), LANES)
    geom = jnp.zeros((LANES, LANES), F32)
    for t in range(4):
        here = jnp.concatenate([pos_ref[t, :, block], jnp.zeros((5, LANES), F32)], axis=0)
        pos_t = here.T
        axis_sum = (
            pos_t[:, 0:1] * lmn_lanes[0:1]
            + pos_t[:, 1:2] * lmn_lanes[1:2]
            + pos_t[:, 2:3] * lmn_lanes[2:3]
        )
        geom = jnp.where(time_of == t, axis_sum, geom)
    geom_blk[...] = geom
    geom = geom_blk[pl.ds(own_at, OWNED), :]

    cos, sin, gain, dual = [], [], [], []
    for fp in range(PAIRS):
        channel = (8 * band + 2 * fp + half).astype(F32)
        turns = (1.0 + channel / F) * geom
        angle = (2.0 * math.pi) * (turns - jnp.round(turns))
        cos.append(jnp.cos(angle))
        sin.append(sign * jnp.sin(angle))
        gain.append(gains_ref[2 * fp : 2 * fp + 2].reshape(LANES, OWNED).T)
        dual.append(duals_ref[2 * fp : 2 * fp + 2].reshape(LANES, OWNED).T)

    def turned(g):
        return [g[i] * cos[i] + swapped(g[i]) * sin[i] for i in range(PAIRS)]

    inv = fit_polynomials()
    quad = []
    for fp in range(PAIRS):
        channel = (8 * band + 2 * fp + half).astype(F32)
        grid = 2.0 * channel / (F - 1) - 1.0
        square = grid * grid
        quad.append([
            jnp.full((1, LANES), float(inv[0, 0]), F32),
            float(inv[1, 1]) * grid,
            float(inv[2, 2]) * square + float(inv[0, 2]),
            grid * (float(inv[3, 3]) * square + float(inv[1, 3])),
        ])

    def fit_start(stage, g, u):
        total = [g[i] + u[i] for i in range(PAIRS)]
        coef = [
            both(sum(quad[i][k] * total[i] for i in range(PAIRS))) for k in range(4)
        ]
        for j in range(2):
            fit_send[stage, j] = jnp.where(low, coef[2 * j], coef[2 * j + 1])
        for k, peer in enumerate(band_peers):
            copy = push(
                fit_send.at[stage], fit_recv.at[stage, k],
                fit_s.at[stage, k], fit_r.at[stage, k], peer,
            )
            copy.start()
            pending.append(copy)

    def fit_finish(stage):
        for k, peer in enumerate(band_peers):
            push(
                fit_send.at[stage], fit_recv.at[stage, k],
                fit_s.at[stage, k], fit_r.at[stage, k], peer,
            ).wait_recv()
        coef = []
        for j in range(2):
            value = fit_send[stage, j]
            for k in range(7):
                value = value + fit_recv[stage, k, j]
            turn = pltpu.roll(value, 64, 1)
            coef += [jnp.where(low, value, turn), jnp.where(low, turn, value)]
        return [sum(quad[i][k] * coef[k] for k in range(4)) for i in range(PAIRS)]

    own_col = 2 * zh + lax.div(y, 2)
    far_col = 2 * (1 - zh) + lax.div(y, 2)
    slot_rows = pl.ds(pl.multiple_of((lax.rem(y, 2) * 4 + x) * OWNED, OWNED), OWNED)
    x_rows = pl.ds(pl.multiple_of(x * OWNED, OWNED), OWNED)
    near = lax.div(x, 2) == zh

    def gather_start(it):
        src = send_buf.at[it]
        copies = [push(src, relay_buf.at[it], rel_s.at[it], rel_r.at[it], at(zh=1 - zh))]
        for k in range(1, 4):
            copies.append(push(
                src, col_buf.at[it, :, slot_rows], own_s.at[it, k],
                col_r.at[it, lax.rem(y, 2) * 4 + x],
                at(y=lax.rem(y + k, 4), x=own_col),
            ))
        for k, peer in enumerate(x_peers):
            copies.append(push(
                src, row_buf.at[it, :, x_rows], row_s.at[it, k], row_r.at[it, k], peer,
            ))
        for copy in copies:
            copy.start()
        pending.extend(copies)
        row_buf[it, :, x_rows, :] = send_buf[it]

    def gather_relay(it):
        push(
            send_buf.at[it], relay_buf.at[it], rel_s.at[it], rel_r.at[it], at(zh=1 - zh)
        ).wait_recv()
        src = relay_buf.at[it]
        for k in range(1, 4):
            copy = push(
                src, col_buf.at[it, :, slot_rows], fwd_s.at[it, k],
                col_r.at[it, lax.rem(y, 2) * 4 + x],
                at(y=lax.rem(y + k, 4), x=far_col),
            )
            copy.start()
            pending.append(copy)

        same_row = push(
            src, col_buf.at[it, :, slot_rows], fwd_s.at[it, 0],
            col_r.at[it, lax.rem(y, 2) * 4 + x], at(x=far_col),
        )

        @pl.when(x != far_col)
        def _():
            same_row.start()

        @pl.when(x == far_col)
        def _():
            col_buf[it, :, slot_rows, :] = relay_buf[it]

    def gather_finish(it):
        for k, peer in enumerate(x_peers):
            push(
                send_buf.at[it], row_buf.at[it, :, x_rows], row_s.at[it, k],
                row_r.at[it, k], peer,
            ).wait_recv()
        for j in range(8):
            from_y = lax.rem(x, 2) * 2 + j // 4
            copy = push(
                send_buf.at[it], col_buf.at[it, :, OWNED * j : OWNED * (j + 1)],
                own_s.at[it, 0], col_r.at[it, j], at(x=lax.rem(x + 1, 4)),
            )
            arrives = jnp.logical_or(
                from_y != y, jnp.logical_and(jnp.logical_not(near), x != j % 4)
            )

            @pl.when(arrives)
            def _(copy=copy):
                copy.wait_recv()

            @pl.when(jnp.logical_and(from_y == y, near))
            def _(j=j):
                col_buf[it, :, OWNED * j : OWNED * (j + 1), :] = row_buf[
                    it, :, OWNED * (j % 4) : OWNED * (j % 4 + 1), :
                ]

    for fp in range(PAIRS):
        send_buf[0, fp] = gain[fp] * cos[fp] + swapped(gain[fp]) * sin[fp]

    pl.semaphore_wait(barrier, 30)
    gather_start(0)
    fit_start(0, gain, dual)

    pair_hot = (
        lax.broadcasted_iota(jnp.int32, (8, LANES), 0)
        == lax.broadcasted_iota(jnp.int32, (8, LANES), 1) // 16
    ).astype(F32)
    col_block = pl.ds(pl.multiple_of(x * LANES, LANES), LANES)
    samples = jnp.zeros((4, 1), F32)
    for fp in range(PAIRS):
        for place, table in ((col_block, flag_col), (block, flag_row)):
            live = jnp.concatenate(
                [flags_ref[2 * fp, :, place], flags_ref[2 * fp + 1, :, place]], axis=0
            ).astype(F32)
            table[fp] = lax.dot_general(
                live, pair_hot, (((0,), (0,)), ((), ())), preferred_element_type=F32
            )
        for f in (2 * fp, 2 * fp + 1):
            count = jnp.sum(flags_ref[f].astype(F32), axis=1, keepdims=True)
            samples = samples + count * (count - 1.0)
    samples = jnp.sum(samples, axis=0, keepdims=True)

    rmat[...] = jnp.zeros_like(rmat)
    gather_relay(0)

    vis_copy.wait()
    row_id = row * 64 + lax.broadcasted_iota(jnp.int32, (64, LANES), 0)
    col_id = x * LANES + lax.broadcasted_iota(jnp.int32, (64, LANES), 1)
    distinct = (row_id != col_id).astype(F32)

    def prepare(fp, carry):
        row_flags = flag_row[fp, pl.ds(row_half, 64), :]
        for f2 in range(2):
            f = 2 * fp + f2
            for t in range(4):
                at_lane = 64 * f2 + 16 * t
                w = row_flags[:, at_lane : at_lane + 1] * distinct
                w = w * flags_ref[f, t : t + 1, col_block].astype(F32)
                weight[f, t] = w
                wvis[f, t, :, 0:LANES] = w * vis_buf[f, t, 0].astype(F32)
                wvis[f, t, :, LANES:] = w * vis_buf[f, t, 1].astype(F32)
        return carry

    lax.fori_loop(0, PAIRS, prepare, 0)

    def products(it):
        def arrange(fp, carry):
            flux = flux_tab[pl.ds(fp, 1), :]
            b = col_buf[it, fp] * flux
            t_buf[it, pl.ds(fp, 1), :] = jnp.sum(b * b * flag_col[fp], axis=0, keepdims=True)
            turned_b = b.T
            p = row_buf[it, fp]
            p_high = p.astype(BF16).astype(F32)
            p_low = p - p_high
            for f2 in range(2):
                f = 2 * fp + f2
                for part, value in ((0, p_high), (64, p_low)):
                    other = pltpu.roll(value, 64, 1)
                    pieces = (value, other) if f2 == 0 else (other, value)
                    lhs[f, part : part + 64, :] = jnp.where(low, *pieces).astype(BF16)
                for t in range(4):
                    start = 64 * f2 + 16 * t
                    left = turned_b[start : start + 16]
                    right = jnp.concatenate([-left[8:16], left[0:8]], axis=0)
                    high, rest = split(jnp.concatenate([left, right], axis=1))
                    rmat[f, t, 16 * t : 16 * t + 16, :] = high
                    rmat[f, t, 64 + 16 * t : 64 + 16 * t + 16, :] = rest
            return carry

        lax.fori_loop(0, PAIRS, arrange, 0)

        def residual(f, squares):
            for t in range(4):
                model = jnp.dot(lhs[f], rmat[f, t], preferred_element_type=F32)
                model = model[0:64] + model[64:128]
                w = weight[f, t]
                r = wvis[f, t] - jnp.concatenate([w, w], axis=1) * model
                high, rest = split(r)
                rhi[f, t, 0:64, :] = high
                rhi[f, t, 64:128, :] = rest
                squares = squares + jnp.sum((r * r).reshape(8, 8, 2 * LANES), axis=0)
            return squares

        squares = lax.fori_loop(0, 8, residual, jnp.zeros((8, 2 * LANES), F32))
        squares = squares[:, 0:LANES] + squares[:, LANES:]
        return jnp.sum(squares, axis=0, keepdims=True)

    def numerators(it):
        def pair(fp, carry):
            halves = []
            for f2 in range(2):
                f = 2 * fp + f2
                total = jnp.zeros((LANES, LANES), F32)
                for t in range(4):
                    total = total + lax.dot_general(
                        rhi[f, t], rmat[f, t], (((1,), (1,)), ((), ())),
                        preferred_element_type=F32,
                    )
                halves.append(both(total[0:64] + total[64:128]))
            num_buf[it, fp] = jnp.where(low, halves[0], halves[1])
            return carry

        lax.fori_loop(0, PAIRS, pair, 0)

    def squares_start(it, stage, value, peers):
        sq_send[it, stage] = value
        for k, peer in enumerate(peers):
            copy = push(
                sq_send.at[it, stage], sq_recv.at[it, stage, k],
                sq_s.at[it, stage, k], sq_r.at[it, stage, k], peer,
            )
            copy.start()
            pending.append(copy)

    def squares_finish(it, stage, peers):
        total = sq_send[it, stage]
        for k, peer in enumerate(peers):
            push(
                sq_send.at[it, stage], sq_recv.at[it, stage, k],
                sq_s.at[it, stage, k], sq_r.at[it, stage, k], peer,
            ).wait_recv()
        for k in range(15):
            total = total + sq_recv[it, stage, k]
        return total

    def exchange_start(it):
        for k, peer in enumerate(x_peers):
            there = lax.rem(x + k + 1, 4)
            rows = pl.ds(pl.multiple_of(there * OWNED, OWNED), OWNED)
            copy = push(
                num_buf.at[it, :, rows], num_recv.at[it, k],
                num_s.at[it, k], num_r.at[it, k], peer,
            )
            copy.start()
            pending.append(copy)

    def exchange_finish(it):
        for k, peer in enumerate(x_peers):
            push(
                num_buf.at[it, :, x_rows], num_recv.at[it, k],
                num_s.at[it, k], num_r.at[it, k], peer,
            ).wait_recv()
            push(t_buf.at[it], t_recv.at[it, k], t_s.at[it, k], t_r.at[it, k], peer).wait_recv()
        num = num_buf[it, :, x_rows, :]
        power = t_buf[it]
        for k in range(3):
            num = num + num_recv[it, k]
            power = power + t_recv[it, k]
        power = power + swapped(power)
        return num, power

    for it in range(ITERS):
        if it > 0:
            gather_relay(it)
        gather_finish(it)
        squares = products(it)
        squares_start(it, 0, squares, plane_peers)
        for k, peer in enumerate(x_peers):
            copy = push(t_buf.at[it], t_recv.at[it, k], t_s.at[it, k], t_r.at[it, k], peer)
            copy.start()
            pending.append(copy)
        numerators(it)
        exchange_start(it)
        squares = squares_finish(it, 0, plane_peers)
        squares = jnp.sum(squares, axis=1, keepdims=True)
        squares_start(it, 1, jnp.where(lane == 0, squares, jnp.where(lane == 1, samples, 0.0)), line_peers)
        smooth = fit_finish(it)
        if it > 0:
            dual = [dual[i] + gain[i] - smooth[i] for i in range(PAIRS)]
        num, power = exchange_finish(it)
        parts = []
        for i in range(PAIRS):
            target = smooth[i] - dual[i]
            mine = send_buf[it, i] * flux_tab[i : i + 1, :]
            mine = mine * mine
            live = flag_row[i, pl.ds(own_at, OWNED), :]
            den = live * (power[i : i + 1] - live * (mine + swapped(mine)))
            numer = num[i] * cos[i] - swapped(num[i]) * sin[i]
            parts.append((numer + den * gain[i], den, target))
        total = squares_finish(it, 1, line_peers)
        count = 0.5 * jnp.sum(jnp.where(lane == 1, total, 0.0), axis=1, keepdims=True)
        total = jnp.sum(jnp.where(lane == 0, total, 0.0), axis=1, keepdims=True)
        rho = PENALTY * S * (total / count + 1e-06)
        gain = [
            0.5 * (gain[i] + (top + rho * target) / (den + rho))
            for i, (top, den, target) in enumerate(parts)
        ]
        if it + 1 < ITERS:
            for i, value in enumerate(turned(gain)):
                send_buf[it + 1, i] = value
            gather_start(it + 1)
        fit_start(it + 1, gain, dual)

    for i in range(PAIRS):
        gains_out[2 * i : 2 * i + 2] = gain[i].T.reshape(2, 4, 2, 8, OWNED)
    smooth = fit_finish(ITERS)
    for i in range(PAIRS):
        value = dual[i] + gain[i] - smooth[i]
        duals_out[2 * i : 2 * i + 2] = value.T.reshape(2, 4, 2, 8, OWNED)

    for copy in pending:
        copy.wait_send()
    for it in range(ITERS):
        same_row = push(
            relay_buf.at[it], col_buf.at[it, :, slot_rows], fwd_s.at[it, 0],
            col_r.at[it, 0], at(x=lax.rem(x + 1, 4)),
        )

        @pl.when(x != far_col)
        def _(same_row=same_row):
            same_row.wait_send()


def shards(vis, flags, positions, lmn, flux, gains, duals):
    vmem = pl.BlockSpec(memory_space=pltpu.VMEM)
    dma = pltpu.SemaphoreType.DMA
    return pl.pallas_call(
        kernel,
        name="admm",
        out_shape=(
            jax.ShapeDtypeStruct(gains.shape, F32),
            jax.ShapeDtypeStruct(duals.shape, F32),
        ),
        in_specs=[pl.BlockSpec(memory_space=pl.ANY)] + [vmem] * 6,
        out_specs=(vmem, vmem),
        scratch_shapes=[
            pltpu.VMEM((8, 4, 2, 64, LANES), BF16),
            pltpu.VMEM((8, 4, 64, 2 * LANES), F32),
            pltpu.VMEM((8, 4, 64, LANES), F32),
            pltpu.VMEM((8, 4, LANES, 2 * LANES), BF16),
            pltpu.VMEM((8, LANES, LANES), BF16),
            pltpu.VMEM((8, 4, LANES, 2 * LANES), BF16),
            pltpu.VMEM((ITERS, PAIRS, 64, LANES), F32),
            pltpu.VMEM((ITERS, PAIRS, LANES, LANES), F32),
            pltpu.VMEM((ITERS, PAIRS, OWNED, LANES), F32),
            pltpu.VMEM((ITERS, PAIRS, OWNED, LANES), F32),
            pltpu.VMEM((ITERS, PAIRS, 64, LANES), F32),
            pltpu.VMEM((ITERS, 3, PAIRS, OWNED, LANES), F32),
            pltpu.VMEM((ITERS, PAIRS, LANES), F32),
            pltpu.VMEM((ITERS, 3, PAIRS, LANES), F32),
            pltpu.VMEM((ITERS + 1, 2, OWNED, LANES), F32),
            pltpu.VMEM((ITERS + 1, 7, 2, OWNED, LANES), F32),
            pltpu.VMEM((ITERS, 2, 1, LANES), F32),
            pltpu.VMEM((ITERS, 2, 15, 1, LANES), F32),
            pltpu.VMEM((PAIRS, LANES, LANES), F32),
            pltpu.VMEM((PAIRS, LANES, LANES), F32),
            pltpu.VMEM((LANES, LANES), F32),
            pltpu.VMEM((PAIRS, LANES), F32),
            dma,
            dma((ITERS, 3)), dma((ITERS, 3)),
            dma((ITERS,)), dma((ITERS,)),
            dma((ITERS, 4)), dma((ITERS, 4)), dma((ITERS, 8)),
            dma((ITERS, 3)), dma((ITERS, 3)),
            dma((ITERS, 3)), dma((ITERS, 3)),
            dma((ITERS, 2, 15)), dma((ITERS, 2, 15)),
            dma((ITERS + 1, 7)), dma((ITERS + 1, 7)),
        ],
        compiler_params=pltpu.CompilerParams(
            collective_id=0, has_side_effects=True, vmem_limit_bytes=48 * 1024 * 1024
        ),
    )(vis, flags, positions, lmn, flux, gains, duals)


def solution(mesh):
    finer = Mesh(mesh.devices.reshape(2, 4, mesh.shape["col"], 4, 2), AXES)
    return jax.shard_map(
        shards,
        mesh=finer,
        in_specs=(
            P(BAND, None, None, ROW, "x"),
            P(BAND, None, None),
            P(),
            P(),
            P(BAND, None),
            P(BAND, None, None, None, OWN),
            P(BAND, None, None, None, OWN),
        ),
        out_specs=(P(BAND, None, None, None, OWN), P(BAND, None, None, None, OWN)),
        check_vma=False,
    )
```

time: 321 us -> 72.2 us (0.22); the launches traced: 316 us -> 71.9 us
  blocking collectives: 114 us -> 0 us
  Pallas kernels: 0 us -> 65.1 us
  matrix products: 52.7 us -> 0 us
  starting transfers between devices: 44.7 us -> 0 us
  local copies, waits for them, and re-layouts: 39.9 us -> 6.14 us
  waiting for transfers between devices: 32.7 us -> 0 us
  other arithmetic: 26.9 us -> 0 us
  between operations: 4.21 us -> 0.68 us
    psum x10 -> x0, blocking collectives: 114 us -> none  [one_axis_at_a_time(): return functools.reduce(lax.psum, axes, array)]
    pallas_call x0 -> x1, Pallas kernels: none -> 65.1 us  [shards(): pl.pallas_call(kernel, name='admm', out_shape=(jax.ShapeDtypeStruct(gains...]
    dot_general x28 -> x0, matrix products: 50.3 us -> none  [the longest x2 9.12 us: shards(): jnp.einsum('ftdp,ftdq->ftpq', row_re, col_im, precision=HIGH)]
    all_to_all x9 -> x0, starting transfers between devices: 44.7 us -> none  [the longest x7 38 us: sent_to_all(): lax.all_to_all(jnp.broadcast_to(array[None], (length, *array.shape)), axi...]
    all_to_all x9 -> x0, waiting for transfers between devices: 32.7 us -> none  [the longest x7 32.7 us: sent_to_all(): lax.all_to_all(jnp.broadcast_to(array[None], (length, *array.shape)), axi...]
    all_to_all x9 -> x0, other arithmetic: 17.3 us -> none  [the longest x7 15 us: sent_to_all(): lax.all_to_all(jnp.broadcast_to(array[None], (length, *array.shape)), axi...]
    unnamed x86 -> x15, local copies, waits for them, and re-layouts: 22.9 us -> 6.14 us
    reshape x9 -> x0, local copies, waits for them, and re-layouts: 5.84 us -> none  [the longest x3 3.61 us: joined_along(): pieces.reshape(*dims[:dim], dims[dim] * dims[dim + 1], *dims[dim + 2:])]
  transfers between devices with their start and end apart: 9 -> 0, of which waited for: 7 -> 0; matrix products, arithmetic and copies ran while one was open for 9% -> 0% of each run, Pallas kernels for 0% -> 0%
where the time goes in v1:
time: 72.2 us; the launch traced here: 71.9 us
  Pallas kernels  65.1 us (90%)
  local copies, waits for them, and re-layouts  6.14 us (9%)
    pallas_call x1, Pallas kernels, shards(): pl.pallas_call(kernel, name='admm', out_shape=(jax.ShapeDtypeStruct(gains...  65.1 us
    unnamed x15, local copies, waits for them, and re-layouts  6.14 us

profile of v1, /device:TPU:1, one launch (start us, length us, event | category | flops | bytes accessed | tf_op | source)
XLA Modules:
  0.0 71.9 jit_solution(9930705355295051138)
XLA Ops:
  0.6 0.0 copy-start.4
  0.6 0.0 copy-start.5
  0.7 0.8 %copy.9.pos_ref = f32[4,3,512]{2,1,0:T(4,128)S(1)} copy(f32[4,3,512]{2,0,1:T(4,128)} %param.9) | data formatting | bytes 49152 | tf_op args[2]
  1.4 0.0 copy-done.4
  1.4 0.0 copy-done.5
  1.4 0.0 copy-start
  1.4 1.2 %copy-done = bf16[8,4,2,64,128]{4,3,2,1,0:T(8,128)(2,1)S(1)} copy-done((bf16[8,4,2,64,128]{4,3,2,1,0:T(8,128)(2,1)S(1)}, bf16[8,4,2,64,128]{4,3,2,1,0:T(8,128)(2,1)}, u32[]{:S(2)}) %copy-start) | copy-done | bytes 1048600
  2.7 0.0 copy-start.1
  2.7 0.9 %copy-done.1 = f32[8,4,2,8,16]{4,3,2,1,0:T(8,128)S(1)} copy-done((f32[8,4,2,8,16]{4,3,2,1,0:T(8,128)S(1)}, f32[8,4,2,8,16]{4,3,2,1,0:T(8,128)}, u32[]{:S(2)}) %copy-start.1) | copy-done | bytes 32792
  3.6 0.0 copy-start.2
  3.6 0.9 %copy-done.2 = f32[8,4,2,8,16]{4,3,2,1,0:T(8,128)S(1)} copy-done((f32[8,4,2,8,16]{4,3,2,1,0:T(8,128)S(1)}, f32[8,4,2,8,16]{4,3,2,1,0:T(8,128)}, u32[]{:S(2)}) %copy-start.2) | copy-done | bytes 32792
  4.6 0.0 copy-start.3
  4.6 0.8 %copy-done.3 = s32[8,4,512]{2,1,0:T(4,128)S(1)} copy-done((s32[8,4,512]{2,1,0:T(4,128)S(1)}, s32[8,4,512]{2,1,0:T(4,128)}, u32[]{:S(2)}) %copy-start.3) | copy-done | bytes 65560
  5.4 65.1 %admm.1 = (f32[8,4,2,8,16]{4,3,2,1,0:T(8,128)S(1)}, f32[8,4,2,8,16]{4,3,2,1,0:T(8,128)S(1)}) custom-call(bf16[8,4,2,64,128]{4,3,2,1,0:T(8,128)(2,1)S(1)} %copy-done, s32[8,4,512]{2,1,0:T(4,128)S(1)} %copy-done.3, f32[4,3,512]{2,1,0:T(4,128)S(1)} %copy.9.pos_ref, f32[3,8]{1,0:T(4,128)S(1)} %copy-done.5, f32[8,8]{1,0:T(8,128)S(1)} %copy-done.4, ...), custom_call_target="tpu_custom_call" | custom-call | tf_op jit(solution)/shard_map/admm/pallas_call | solution.py:484
  70.5 0.7 copy.12
  71.2 0.7 copy.13
Async XLA Ops:
  0.6 0.8 %copy-start.4 = (f32[8,8]{1,0:T(8,128)S(1)}, f32[8,8]{1,0:T(8,128)}, u32[]{:S(2)}) copy-start(f32[8,8]{1,0:T(8,128)} %flux_ref.1) | copy-start | bytes 772
  0.6 0.8 %copy-start.5 = (f32[3,8]{1,0:T(4,128)S(1)}, f32[3,8]{1,0:T(4,128)}, u32[]{:S(2)}) copy-start(f32[3,8]{1,0:T(4,128)} %lmn_ref.1) | copy-start | bytes 292
  1.4 1.2 %copy-start = (bf16[8,4,2,64,128]{4,3,2,1,0:T(8,128)(2,1)S(1)}, bf16[8,4,2,64,128]{4,3,2,1,0:T(8,128)(2,1)}, u32[]{:S(2)}) copy-start(bf16[8,4,2,64,128]{4,3,2,1,0:T(8,128)(2,1)} %vis_hbm.1) | copy-start | bytes 3145732
  2.7 0.9 %copy-start.1 = (f32[8,4,2,8,16]{4,3,2,1,0:T(8,128)S(1)}, f32[8,4,2,8,16]{4,3,2,1,0:T(8,128)}, u32[]{:S(2)}) copy-start(f32[8,4,2,8,16]{4,3,2,1,0:T(8,128)} %gains_ref.1) | copy-start | bytes 98308
  3.6 0.9 %copy-start.2 = (f32[8,4,2,8,16]{4,3,2,1,0:T(8,128)S(1)}, f32[8,4,2,8,16]{4,3,2,1,0:T(8,128)}, u32[]{:S(2)}) copy-start(f32[8,4,2,8,16]{4,3,2,1,0:T(8,128)} %duals_ref.1) | copy-start | bytes 98308
  4.6 0.8 %copy-start.3 = (s32[8,4,512]{2,1,0:T(4,128)S(1)}, s32[8,4,512]{2,1,0:T(4,128)}, u32[]{:S(2)}) copy-start(s32[8,4,512]{2,1,0:T(4,128)} %flags_ref.1) | copy-start | bytes 196612

commit v2 on v1

--- a/solution.py
+++ b/solution.py
@@ -23,6 +23,8 @@
 F32 = jnp.float32
 BF16 = jnp.bfloat16
 PAIRS = 4
+CHUNKS = 2
+GATHERS = 3
 OWNED = 16
 LANES = 128
 
@@ -40,13 +42,13 @@
 
 
 def kernel(
-    vis_hbm, flags_ref, pos_ref, lmn_ref, flux_ref, gains_ref, duals_ref,
+    vis_hbm, flags_hbm, pos_hbm, lmn_hbm, flux_hbm, gains_hbm, duals_hbm,
     gains_out, duals_out,
-    vis_buf, wvis, weight, rmat, lhs, rhi,
+    vis_buf, flags_ref, pos_ref, lmn_ref, flux_ref, gains_ref, duals_ref, wvis, weight, rmat, lhs, rhi,
     row_buf, col_buf, relay_buf, send_buf, num_buf, num_recv,
     t_buf, t_recv, fit_send, fit_recv, sq_send, sq_recv,
     flag_col, flag_row, geom_blk, flux_tab,
-    vis_sem, row_s, row_r, rel_s, rel_r, own_s, fwd_s, col_r,
+    in_sem, row_s, row_r, rel_s, rel_r, own_s, fwd_s, col_r,
     num_s, num_r, t_s, t_r, sq_s, sq_r, fit_s, fit_r,
 ):
     me = {axis: lax.axis_index(axis) for axis in AXES}
@@ -79,11 +81,20 @@
 
     pending = []
 
+    gains_copy, pos_copy, lmn_copy, flux_copy, duals_copy, flags_copy, vis_copy = (
+        pltpu.make_async_copy(src, dst, in_sem.at[i])
+        for i, (src, dst) in enumerate((
+            (gains_hbm, gains_ref), (pos_hbm, pos_ref), (lmn_hbm, lmn_ref),
+            (flux_hbm, flux_ref), (duals_hbm, duals_ref), (flags_hbm, flags_ref),
+            (vis_hbm, vis_buf),
+        ))
+    )
+    for copy in (gains_copy, pos_copy, lmn_copy, flux_copy, duals_copy, flags_copy, vis_copy):
+        copy.start()
+
     barrier = pltpu.get_barrier_semaphore()
     for peer in plane_peers + line_peers:
         pl.semaphore_signal(barrier, inc=1, device_id=peer, device_id_type=MESH)
-    vis_copy = pltpu.make_async_copy(vis_hbm, vis_buf, vis_sem)
-    vis_copy.start()
 
     lane = lax.broadcasted_iota(jnp.int32, (1, LANES), 1)
     half = lane // 64
@@ -107,27 +118,29 @@
         lax.broadcasted_iota(jnp.int32, (8, LANES), 0)
         == lax.broadcasted_iota(jnp.int32, (8, LANES), 1) % 8
     ).astype(F32)
-    flux_all = jnp.dot(flux_ref[...], dir_hot, precision=HIGH, preferred_element_type=F32)
-    for fp in range(PAIRS):
-        flux_tab[pl.ds(fp, 1), :] = jnp.where(
-            low, flux_all[2 * fp : 2 * fp + 1], flux_all[2 * fp + 1 : 2 * fp + 2]
-        )
-    lmn_lanes = jnp.dot(lmn_ref[...], dir_hot, precision=HIGH, preferred_element_type=F32)
     time_of = (lane // 16) % 4
     block = pl.ds(pl.multiple_of(row_block * LANES, LANES), LANES)
+    pos_copy.wait()
+    lmn_copy.wait()
+    lmn_lanes = jnp.dot(lmn_ref[...], dir_hot, precision=HIGH, preferred_element_type=F32)
+    places = jnp.concatenate(
+        [pos_ref[k, :, block] for k in range(3)] + [jnp.zeros((4, LANES), F32)], axis=0
+    ).T
     geom = jnp.zeros((LANES, LANES), F32)
     for t in range(4):
-        here = jnp.concatenate([pos_ref[t, :, block], jnp.zeros((5, LANES), F32)], axis=0)
-        pos_t = here.T
         axis_sum = (
-            pos_t[:, 0:1] * lmn_lanes[0:1]
-            + pos_t[:, 1:2] * lmn_lanes[1:2]
-            + pos_t[:, 2:3] * lmn_lanes[2:3]
+            places[:, t : t + 1] * lmn_lanes[0:1]
+            + places[:, t + 4 : t + 5] * lmn_lanes[1:2]
+            + places[:, t + 8 : t + 9] * lmn_lanes[2:3]
         )
         geom = jnp.where(time_of == t, axis_sum, geom)
     geom_blk[...] = geom
     geom = geom_blk[pl.ds(own_at, OWNED), :]
 
+    def turned(g, i):
+        return g * cos[i] + swapped(g) * sin[i]
+
+    gains_copy.wait()
     cos, sin, gain, dual = [], [], [], []
     for fp in range(PAIRS):
         channel = (8 * band + 2 * fp + half).astype(F32)
@@ -136,10 +149,10 @@
         cos.append(jnp.cos(angle))
         sin.append(sign * jnp.sin(angle))
         gain.append(gains_ref[2 * fp : 2 * fp + 2].reshape(LANES, OWNED).T)
+        send_buf[0, fp] = turned(gain[fp], fp)
+    duals_copy.wait()
+    for fp in range(PAIRS):
         dual.append(duals_ref[2 * fp : 2 * fp + 2].reshape(LANES, OWNED).T)
-
-    def turned(g):
-        return [g[i] * cos[i] + swapped(g[i]) * sin[i] for i in range(PAIRS)]
 
     inv = fit_polynomials()
     quad = []
@@ -190,62 +203,76 @@
     x_rows = pl.ds(pl.multiple_of(x * OWNED, OWNED), OWNED)
     near = lax.div(x, 2) == zh
 
-    def gather_start(it):
-        src = send_buf.at[it]
-        copies = [push(src, relay_buf.at[it], rel_s.at[it], rel_r.at[it], at(zh=1 - zh))]
-        for k in range(1, 4):
-            copies.append(push(
-                src, col_buf.at[it, :, slot_rows], own_s.at[it, k],
-                col_r.at[it, lax.rem(y, 2) * 4 + x],
-                at(y=lax.rem(y + k, 4), x=own_col),
-            ))
+    own_slot = lax.rem(y, 2) * 4 + x
+
+    def part(h):
+        return pl.ds(h * (PAIRS // CHUNKS), PAIRS // CHUNKS)
+
+    def across(slot, h):
+        return push(
+            send_buf.at[slot, part(h)], relay_buf.at[slot, part(h)],
+            rel_s.at[slot, h], rel_r.at[slot, h], at(zh=1 - zh),
+        )
+
+    def gather_start(slot):
+        copies = [across(slot, h) for h in range(CHUNKS)]
         for k, peer in enumerate(x_peers):
             copies.append(push(
-                src, row_buf.at[it, :, x_rows], row_s.at[it, k], row_r.at[it, k], peer,
+                send_buf.at[slot], row_buf.at[slot, :, x_rows],
+                row_s.at[slot, k], row_r.at[slot, k], peer,
             ))
+        for h in range(CHUNKS):
+            for k in range(1, 4):
+                copies.append(push(
+                    send_buf.at[slot, part(h)], col_buf.at[slot, part(h), slot_rows],
+                    own_s.at[slot, k, h], col_r.at[slot, own_slot, h],
+                    at(y=lax.rem(y + k, 4), x=own_col),
+                ))
         for copy in copies:
             copy.start()
         pending.extend(copies)
-        row_buf[it, :, x_rows, :] = send_buf[it]
-
-    def gather_relay(it):
-        push(
-            send_buf.at[it], relay_buf.at[it], rel_s.at[it], rel_r.at[it], at(zh=1 - zh)
-        ).wait_recv()
-        src = relay_buf.at[it]
-        for k in range(1, 4):
-            copy = push(
-                src, col_buf.at[it, :, slot_rows], fwd_s.at[it, k],
-                col_r.at[it, lax.rem(y, 2) * 4 + x],
-                at(y=lax.rem(y + k, 4), x=far_col),
-            )
-            copy.start()
-            pending.append(copy)
-
-        same_row = push(
-            src, col_buf.at[it, :, slot_rows], fwd_s.at[it, 0],
-            col_r.at[it, lax.rem(y, 2) * 4 + x], at(x=far_col),
+        row_buf[slot, :, x_rows, :] = send_buf[slot]
+
+    def to_far_col(slot, h):
+        return push(
+            relay_buf.at[slot, part(h)], col_buf.at[slot, part(h), slot_rows],
+            fwd_s.at[slot, 0, h], col_r.at[slot, own_slot, h], at(x=far_col),
         )
 
-        @pl.when(x != far_col)
-        def _():
-            same_row.start()
-
-        @pl.when(x == far_col)
-        def _():
-            col_buf[it, :, slot_rows, :] = relay_buf[it]
-
-    def gather_finish(it):
-        for k, peer in enumerate(x_peers):
-            push(
-                send_buf.at[it], row_buf.at[it, :, x_rows], row_s.at[it, k],
-                row_r.at[it, k], peer,
-            ).wait_recv()
+    def gather_relay(slot):
+        for h in range(CHUNKS):
+            across(slot, h).wait_recv()
+            for k in range(1, 4):
+                copy = push(
+                    relay_buf.at[slot, part(h)], col_buf.at[slot, part(h), slot_rows],
+                    fwd_s.at[slot, k, h], col_r.at[slot, own_slot, h],
+                    at(y=lax.rem(y + k, 4), x=far_col),
+                )
+                copy.start()
+                pending.append(copy)
+
+            @pl.when(x != far_col)
+            def _(h=h):
+                to_far_col(slot, h).start()
+
+            @pl.when(x == far_col)
+            def _(h=h):
+                col_buf[slot, part(h), slot_rows, :] = relay_buf[slot, part(h)]
+
+    def gather_finish(slot, h):
+        if h == 0:
+            for k, peer in enumerate(x_peers):
+                push(
+                    send_buf.at[slot], row_buf.at[slot, :, x_rows],
+                    row_s.at[slot, k], row_r.at[slot, k], peer,
+                ).wait_recv()
         for j in range(8):
             from_y = lax.rem(x, 2) * 2 + j // 4
+            rows = slice(OWNED * j, OWNED * (j + 1))
+            row_rows = slice(OWNED * (j % 4), OWNED * (j % 4 + 1))
             copy = push(
-                send_buf.at[it], col_buf.at[it, :, OWNED * j : OWNED * (j + 1)],
-                own_s.at[it, 0], col_r.at[it, j], at(x=lax.rem(x + 1, 4)),
+                send_buf.at[slot, part(h)], col_buf.at[slot, part(h), rows],
+                own_s.at[slot, 0, h], col_r.at[slot, j, h], x_peers[0],
             )
             arrives = jnp.logical_or(
                 from_y != y, jnp.logical_and(jnp.logical_not(near), x != j % 4)
@@ -256,17 +283,19 @@
                 copy.wait_recv()
 
             @pl.when(jnp.logical_and(from_y == y, near))
-            def _(j=j):
-                col_buf[it, :, OWNED * j : OWNED * (j + 1), :] = row_buf[
-                    it, :, OWNED * (j % 4) : OWNED * (j % 4 + 1), :
-                ]
-
-    for fp in range(PAIRS):
-        send_buf[0, fp] = gain[fp] * cos[fp] + swapped(gain[fp]) * sin[fp]
+            def _(rows=rows, row_rows=row_rows):
+                col_buf[slot, part(h), rows, :] = row_buf[slot, part(h), row_rows, :]
 
     pl.semaphore_wait(barrier, 30)
     gather_start(0)
     fit_start(0, gain, dual)
+
+    flux_copy.wait()
+    flux_all = jnp.dot(flux_ref[...], dir_hot, precision=HIGH, preferred_element_type=F32)
+    for fp in range(PAIRS):
+        flux_tab[pl.ds(fp, 1), :] = jnp.where(
+            low, flux_all[2 * fp : 2 * fp + 1], flux_all[2 * fp + 1 : 2 * fp + 2]
+        )
 
     pair_hot = (
         lax.broadcasted_iota(jnp.int32, (8, LANES), 0)
@@ -274,6 +303,7 @@
     ).astype(F32)
     col_block = pl.ds(pl.multiple_of(x * LANES, LANES), LANES)
     samples = jnp.zeros((4, 1), F32)
+    flags_copy.wait()
     for fp in range(PAIRS):
         for place, table in ((col_block, flag_col), (block, flag_row)):
             live = jnp.concatenate(
@@ -289,6 +319,10 @@
 
     rmat[...] = jnp.zeros_like(rmat)
     gather_relay(0)
+    smooth = fit_finish(0)
+    for i in range(PAIRS):
+        send_buf[1, i] = turned(smooth[i] - dual[i], i)
+    gather_start(1)
 
     vis_copy.wait()
     row_id = row * 64 + lax.broadcasted_iota(jnp.int32, (64, LANES), 0)
@@ -310,32 +344,33 @@
 
     lax.fori_loop(0, PAIRS, prepare, 0)
 
+    def arrange(it, fp):
+        flux = flux_tab[pl.ds(fp, 1), :]
+        b = col_buf[0, fp]
+        p = row_buf[0, fp]
+        if it > 0:
+            b = b + col_buf[1, fp] * col_buf[2, fp]
+            p = p + row_buf[1, fp] * row_buf[2, fp]
+        b = b * flux
+        t_buf[it, pl.ds(fp, 1), :] = jnp.sum(b * b * flag_col[fp], axis=0, keepdims=True)
+        turned_b = b.T
+        p_high = p.astype(BF16).astype(F32)
+        p_low = p - p_high
+        for f2 in range(2):
+            f = 2 * fp + f2
+            for start, value in ((0, p_high), (64, p_low)):
+                other = pltpu.roll(value, 64, 1)
+                pieces = (value, other) if f2 == 0 else (other, value)
+                lhs[f, start : start + 64, :] = jnp.where(low, *pieces).astype(BF16)
+            for t in range(4):
+                start = 64 * f2 + 16 * t
+                left = turned_b[start : start + 16]
+                right = jnp.concatenate([-left[8:16], left[0:8]], axis=0)
+                high, rest = split(jnp.concatenate([left, right], axis=1))
+                rmat[f, t, 16 * t : 16 * t + 16, :] = high
+                rmat[f, t, 64 + 16 * t : 64 + 16 * t + 16, :] = rest
+
     def products(it):
-        def arrange(fp, carry):
-            flux = flux_tab[pl.ds(fp, 1), :]
-            b = col_buf[it, fp] * flux
-            t_buf[it, pl.ds(fp, 1), :] = jnp.sum(b * b * flag_col[fp], axis=0, keepdims=True)
-            turned_b = b.T
-            p = row_buf[it, fp]
-            p_high = p.astype(BF16).astype(F32)
-            p_low = p - p_high
-            for f2 in range(2):
-                f = 2 * fp + f2
-                for part, value in ((0, p_high), (64, p_low)):
-                    other = pltpu.roll(value, 64, 1)
-                    pieces = (value, other) if f2 == 0 else (other, value)
-                    lhs[f, part : part + 64, :] = jnp.where(low, *pieces).astype(BF16)
-                for t in range(4):
-                    start = 64 * f2 + 16 * t
-                    left = turned_b[start : start + 16]
-                    right = jnp.concatenate([-left[8:16], left[0:8]], axis=0)
-                    high, rest = split(jnp.concatenate([left, right], axis=1))
-                    rmat[f, t, 16 * t : 16 * t + 16, :] = high
-                    rmat[f, t, 64 + 16 * t : 64 + 16 * t + 16, :] = rest
-            return carry
-
-        lax.fori_loop(0, PAIRS, arrange, 0)
-
         def residual(f, squares):
             for t in range(4):
                 model = jnp.dot(lhs[f], rmat[f, t], preferred_element_type=F32)
@@ -348,7 +383,17 @@
                 squares = squares + jnp.sum((r * r).reshape(8, 8, 2 * LANES), axis=0)
             return squares
 
-        squares = lax.fori_loop(0, 8, residual, jnp.zeros((8, 2 * LANES), F32))
+        squares = jnp.zeros((8, 2 * LANES), F32)
+        for h in range(CHUNKS):
+            gather_finish(2 * it, h)
+            first, end = h * PAIRS // CHUNKS, (h + 1) * PAIRS // CHUNKS
+
+            def arranged(fp, carry):
+                arrange(it, fp)
+                return carry
+
+            lax.fori_loop(first, end, arranged, 0)
+            squares = lax.fori_loop(2 * first, 2 * end, residual, squares)
         squares = squares[:, 0:LANES] + squares[:, LANES:]
         return jnp.sum(squares, axis=0, keepdims=True)
 
@@ -416,10 +461,12 @@
         power = power + swapped(power)
         return num, power
 
+    def solve_for(p, live, flux, power):
+        b = p * flux
+        b = b * b
+        return live * (power - live * (b + swapped(b)))
+
     for it in range(ITERS):
-        if it > 0:
-            gather_relay(it)
-        gather_finish(it)
         squares = products(it)
         squares_start(it, 0, squares, plane_peers)
         for k, peer in enumerate(x_peers):
@@ -428,20 +475,30 @@
             pending.append(copy)
         numerators(it)
         exchange_start(it)
+        if it == 0:
+            gather_relay(1)
+            num, power = exchange_finish(it)
+            send_buf[2] = num
+            gather_start(2)
         squares = squares_finish(it, 0, plane_peers)
         squares = jnp.sum(squares, axis=1, keepdims=True)
-        squares_start(it, 1, jnp.where(lane == 0, squares, jnp.where(lane == 1, samples, 0.0)), line_peers)
-        smooth = fit_finish(it)
-        if it > 0:
+        squares_start(
+            it, 1,
+            jnp.where(lane == 0, squares, jnp.where(lane == 1, samples, 0.0)), line_peers,
+        )
+        if it == 0:
+            gather_relay(2)
+        else:
+            smooth = fit_finish(it)
             dual = [dual[i] + gain[i] - smooth[i] for i in range(PAIRS)]
-        num, power = exchange_finish(it)
+            num, power = exchange_finish(it)
         parts = []
         for i in range(PAIRS):
             target = smooth[i] - dual[i]
-            mine = send_buf[it, i] * flux_tab[i : i + 1, :]
-            mine = mine * mine
             live = flag_row[i, pl.ds(own_at, OWNED), :]
-            den = live * (power[i : i + 1] - live * (mine + swapped(mine)))
+            den = solve_for(
+                turned(gain[i], i), live, flux_tab[i : i + 1, :], power[i : i + 1]
+            )
             numer = num[i] * cos[i] - swapped(num[i]) * sin[i]
             parts.append((numer + den * gain[i], den, target))
         total = squares_finish(it, 1, line_peers)
@@ -452,11 +509,21 @@
             0.5 * (gain[i] + (top + rho * target) / (den + rho))
             for i, (top, den, target) in enumerate(parts)
         ]
+        fit_start(it + 1, gain, dual)
         if it + 1 < ITERS:
-            for i, value in enumerate(turned(gain)):
-                send_buf[it + 1, i] = value
-            gather_start(it + 1)
-        fit_start(it + 1, gain, dual)
+            for h in range(CHUNKS):
+                gather_finish(1, h)
+            for i in range(PAIRS):
+                flux, every = flux_tab[i : i + 1, :], power[i : i + 1]
+                for buf, live in (
+                    (row_buf, flag_row[i, pl.ds(row_half, 64), :]),
+                    (col_buf, flag_col[i]),
+                ):
+                    p = buf[0, i]
+                    den = solve_for(p, live, flux, every)
+                    share = 0.5 / (den + rho)
+                    buf[0, i] = 0.5 * p + share * (den * p + rho * buf[1, i])
+                    buf[1, i] = share
 
     for i in range(PAIRS):
         gains_out[2 * i : 2 * i + 2] = gain[i].T.reshape(2, 4, 2, 8, OWNED)
@@ -467,19 +534,17 @@
 
     for copy in pending:
         copy.wait_send()
-    for it in range(ITERS):
-        same_row = push(
-            relay_buf.at[it], col_buf.at[it, :, slot_rows], fwd_s.at[it, 0],
-            col_r.at[it, 0], at(x=lax.rem(x + 1, 4)),
-        )
-
-        @pl.when(x != far_col)
-        def _(same_row=same_row):
-            same_row.wait_send()
+
+    @pl.when(x != far_col)
+    def _():
+        for slot in range(GATHERS):
+            for h in range(CHUNKS):
+                to_far_col(slot, h).wait_send()
 
 
 def shards(vis, flags, positions, lmn, flux, gains, duals):
     vmem = pl.BlockSpec(memory_space=pltpu.VMEM)
+    positions = jnp.swapaxes(positions, 0, 1)
     dma = pltpu.SemaphoreType.DMA
     return pl.pallas_call(
         kernel,
@@ -488,19 +553,25 @@
             jax.ShapeDtypeStruct(gains.shape, F32),
             jax.ShapeDtypeStruct(duals.shape, F32),
         ),
-        in_specs=[pl.BlockSpec(memory_space=pl.ANY)] + [vmem] * 6,
+        in_specs=[pl.BlockSpec(memory_space=pltpu.HBM)] * 7,
         out_specs=(vmem, vmem),
         scratch_shapes=[
-            pltpu.VMEM((8, 4, 2, 64, LANES), BF16),
+            pltpu.VMEM(vis.shape, BF16),
+            pltpu.VMEM(flags.shape, jnp.int32),
+            pltpu.VMEM(positions.shape, F32),
+            pltpu.VMEM(lmn.shape, F32),
+            pltpu.VMEM(flux.shape, F32),
+            pltpu.VMEM(gains.shape, F32),
+            pltpu.VMEM(duals.shape, F32),
             pltpu.VMEM((8, 4, 64, 2 * LANES), F32),
             pltpu.VMEM((8, 4, 64, LANES), F32),
             pltpu.VMEM((8, 4, LANES, 2 * LANES), BF16),
             pltpu.VMEM((8, LANES, LANES), BF16),
             pltpu.VMEM((8, 4, LANES, 2 * LANES), BF16),
-            pltpu.VMEM((ITERS, PAIRS, 64, LANES), F32),
-            pltpu.VMEM((ITERS, PAIRS, LANES, LANES), F32),
-            pltpu.VMEM((ITERS, PAIRS, OWNED, LANES), F32),
-            pltpu.VMEM((ITERS, PAIRS, OWNED, LANES), F32),
+            pltpu.VMEM((GATHERS, PAIRS, 64, LANES), F32),
+            pltpu.VMEM((GATHERS, PAIRS, LANES, LANES), F32),
+            pltpu.VMEM((GATHERS, PAIRS, OWNED, LANES), F32),
+            pltpu.VMEM((GATHERS, PAIRS, OWNED, LANES), F32),
             pltpu.VMEM((ITERS, PAIRS, 64, LANES), F32),
             pltpu.VMEM((ITERS, 3, PAIRS, OWNED, LANES), F32),
             pltpu.VMEM((ITERS, PAIRS, LANES), F32),
@@ -513,17 +584,18 @@
             pltpu.VMEM((PAIRS, LANES, LANES), F32),
             pltpu.VMEM((LANES, LANES), F32),
             pltpu.VMEM((PAIRS, LANES), F32),
-            dma,
-            dma((ITERS, 3)), dma((ITERS, 3)),
-            dma((ITERS,)), dma((ITERS,)),
-            dma((ITERS, 4)), dma((ITERS, 4)), dma((ITERS, 8)),
+            dma((7,)),
+            dma((GATHERS, 3)), dma((GATHERS, 3)),
+            dma((GATHERS, CHUNKS)), dma((GATHERS, CHUNKS)),
+            dma((GATHERS, 4, CHUNKS)), dma((GATHERS, 4, CHUNKS)),
+            dma((GATHERS, 8, CHUNKS)),
             dma((ITERS, 3)), dma((ITERS, 3)),
             dma((ITERS, 3)), dma((ITERS, 3)),
             dma((ITERS, 2, 15)), dma((ITERS, 2, 15)),
             dma((ITERS + 1, 7)), dma((ITERS + 1, 7)),
         ],
         compiler_params=pltpu.CompilerParams(
-            collective_id=0, has_side_effects=True, vmem_limit_bytes=48 * 1024 * 1024
+            collective_id=0, has_side_effects=True, vmem_limit_bytes=60 * 1024 * 1024
         ),
     )(vis, flags, positions, lmn, flux, gains, duals)
 

time: 72.2 us -> 64.9 us (0.90)
  local copies, waits for them, and re-layouts: 6.14 us -> 2.42 us
  Pallas kernels: 65.1 us -> 61.7 us
    unnamed x15 -> x4, local copies, waits for them, and re-layouts: 6.14 us -> 2.42 us
    pallas_call x1, Pallas kernels: 65.1 us -> 61.7 us  [shards(): pl.pallas_call(kernel, name='admm', out_shape=(jax.ShapeDtypeStruct(gains...]
where the time goes in v2:
time: 64.9 us; the launch traced here: 64.8 us
  Pallas kernels  61.7 us (95%)
  local copies, waits for them, and re-layouts  2.42 us (4%)
  between operations  0.65 us (1%)
    pallas_call x1, Pallas kernels, shards(): pl.pallas_call(kernel, name='admm', out_shape=(jax.ShapeDtypeStruct(gains...  61.7 us
    unnamed x4, local copies, waits for them, and re-layouts  2.42 us

profile of v2, /device:TPU:1, one launch (start us, length us, event | category | flops | bytes accessed | tf_op | source)
XLA Modules:
  0.0 64.8 jit_solution(16606731774793787558)
XLA Ops:
  0.6 61.7 %admm.1 = (f32[8,4,2,8,16]{4,3,2,1,0:T(8,128)}, f32[8,4,2,8,16]{4,3,2,1,0:T(8,128)}) custom-call(bf16[8,4,2,64,128]{4,3,2,1,0:T(8,128)(2,1)} %vis_hbm.1, s32[8,4,512]{2,1,0:T(4,128)} %flags_hbm.1, f32[3,4,512]{2,1,0:T(4,128)} %bitcast.1, f32[3,8]{1,0:T(4,128)} %lmn_hbm.1, f32[8,8]{1,0:T(8,128)} %flux_hbm.1, f32[8,4,2,8,16]{4,3,2,1,0:T(8,128)} %gains_hbm.1, ...), custom_call_target="tpu_custom_call" | custom-call | tf_op jit(solution)/shard_map/admm/pallas_call | solution.py:549
  62.4 0.0 copy-start
  62.4 1.7 %copy.11 = f32[8,4,2,8,16]{4,3,2,1,0:T(8,128)} copy(f32[8,4,2,8,16]{4,3,2,1,0:T(8,128)} %get-tuple-element.4) | data formatting | bytes 65536
  64.1 0.0 copy-done
  64.1 0.7 %copy.12 = f32[8,4,2,8,16]{4,3,2,1,0:T(8,128)} copy(f32[8,4,2,8,16]{4,3,2,1,0:T(8,128)S(1)} %copy-done) | data formatting | bytes 65536
Async XLA Ops:
  62.4 1.7 %copy-start = (f32[8,4,2,8,16]{4,3,2,1,0:T(8,128)S(1)}, f32[8,4,2,8,16]{4,3,2,1,0:T(8,128)}, u32[]{:S(2)}) copy-start(f32[8,4,2,8,16]{4,3,2,1,0:T(8,128)} %get-tuple-element.5) | copy-start | bytes 98308

commit v3 on v2

--- a/solution.py
+++ b/solution.py
@@ -23,8 +23,9 @@
 F32 = jnp.float32
 BF16 = jnp.bfloat16
 PAIRS = 4
-CHUNKS = 2
-GATHERS = 3
+CHUNKS = 1
+GATHERS = 2
+CROSSED = 3
 OWNED = 16
 LANES = 128
 
@@ -43,11 +44,11 @@
 
 def kernel(
     vis_hbm, flags_hbm, pos_hbm, lmn_hbm, flux_hbm, gains_hbm, duals_hbm,
-    gains_out, duals_out,
-    vis_buf, flags_ref, pos_ref, lmn_ref, flux_ref, gains_ref, duals_ref, wvis, weight, rmat, lhs, rhi,
+    solved,
+    vis_buf, flags_ref, pos_ref, lmn_ref, flux_ref, gains_ref, duals_ref, wvis, weight, rmat, lhs, resid,
     row_buf, col_buf, relay_buf, send_buf, num_buf, num_recv,
     t_buf, t_recv, fit_send, fit_recv, sq_send, sq_recv,
-    flag_col, flag_row, geom_blk, flux_tab,
+    flag_col, flag_row, flag_tmp, flag_far, new_p, far_p, geom_blk, flux_tab,
     in_sem, row_s, row_r, rel_s, rel_r, own_s, fwd_s, col_r,
     num_s, num_r, t_s, t_r, sq_s, sq_r, fit_s, fit_r,
 ):
@@ -72,6 +73,8 @@
         for k in range(1, 16)
     ]
     band_peers = line_peers[:7]
+    plane_order = (9, 8, 10, 5, 13, 7, 1, 6, 4, 14, 12, 0, 2, 3, 11)
+    line_order = (7, 8, 9, 10, 11, 12, 13, 14, 3, 4, 5, 6, 1, 2, 0)
 
     def push(src, dst, send_sem, recv_sem, device):
         return pltpu.make_async_remote_copy(
@@ -93,7 +96,7 @@
         copy.start()
 
     barrier = pltpu.get_barrier_semaphore()
-    for peer in plane_peers + line_peers:
+    for peer in [line_peers[k] for k in line_order] + [plane_peers[k] for k in plane_order]:
         pl.semaphore_signal(barrier, inc=1, device_id=peer, device_id_type=MESH)
 
     lane = lax.broadcasted_iota(jnp.int32, (1, LANES), 1)
@@ -214,56 +217,67 @@
             rel_s.at[slot, h], rel_r.at[slot, h], at(zh=1 - zh),
         )
 
-    def gather_start(slot):
-        copies = [across(slot, h) for h in range(CHUNKS)]
-        for k, peer in enumerate(x_peers):
-            copies.append(push(
-                send_buf.at[slot], row_buf.at[slot, :, x_rows],
-                row_s.at[slot, k], row_r.at[slot, k], peer,
-            ))
+    def cross(slot):
         for h in range(CHUNKS):
-            for k in range(1, 4):
+            copy = across(slot, h)
+            copy.start()
+            pending.append(copy)
+
+    def crossed(slot):
+        for h in range(CHUNKS):
+            across(slot, h).wait_recv()
+
+    def spread(slot, src):
+        copies = []
+        for h in range(CHUNKS):
+            for k in (2, 1, 3):
                 copies.append(push(
-                    send_buf.at[slot, part(h)], col_buf.at[slot, part(h), slot_rows],
+                    src.at[part(h)], col_buf.at[slot, part(h), slot_rows],
                     own_s.at[slot, k, h], col_r.at[slot, own_slot, h],
                     at(y=lax.rem(y + k, 4), x=own_col),
                 ))
         for copy in copies:
             copy.start()
         pending.extend(copies)
-        row_buf[slot, :, x_rows, :] = send_buf[slot]
-
-    def to_far_col(slot, h):
+
+    def spread_row(slot, src):
+        for k, peer in enumerate(x_peers):
+            copy = push(
+                src, row_buf.at[slot, :, x_rows], row_s.at[slot, k], row_r.at[slot, k], peer,
+            )
+            copy.start()
+            pending.append(copy)
+        row_buf[slot, :, x_rows, :] = src[...]
+
+    def to_far_col(slot, src, h):
         return push(
-            relay_buf.at[slot, part(h)], col_buf.at[slot, part(h), slot_rows],
+            src.at[part(h)], col_buf.at[slot, part(h), slot_rows],
             fwd_s.at[slot, 0, h], col_r.at[slot, own_slot, h], at(x=far_col),
         )
 
-    def gather_relay(slot):
-        for h in range(CHUNKS):
-            across(slot, h).wait_recv()
-            for k in range(1, 4):
-                copy = push(
-                    relay_buf.at[slot, part(h)], col_buf.at[slot, part(h), slot_rows],
-                    fwd_s.at[slot, k, h], col_r.at[slot, own_slot, h],
-                    at(y=lax.rem(y + k, 4), x=far_col),
-                )
-                copy.start()
-                pending.append(copy)
-
-            @pl.when(x != far_col)
-            def _(h=h):
-                to_far_col(slot, h).start()
-
-            @pl.when(x == far_col)
-            def _(h=h):
-                col_buf[slot, part(h), slot_rows, :] = relay_buf[slot, part(h)]
+    def relay(slot, src, h):
+        for k in range(1, 4):
+            copy = push(
+                src.at[part(h)], col_buf.at[slot, part(h), slot_rows],
+                fwd_s.at[slot, k, h], col_r.at[slot, own_slot, h],
+                at(y=lax.rem(y + k, 4), x=far_col),
+            )
+            copy.start()
+            pending.append(copy)
+
+        @pl.when(x != far_col)
+        def _():
+            to_far_col(slot, src, h).start()
+
+        @pl.when(x == far_col)
+        def _():
+            col_buf[slot, part(h), slot_rows, :] = src[part(h)]
 
     def gather_finish(slot, h):
         if h == 0:
             for k, peer in enumerate(x_peers):
                 push(
-                    send_buf.at[slot], row_buf.at[slot, :, x_rows],
+                    new_p, row_buf.at[slot, :, x_rows],
                     row_s.at[slot, k], row_r.at[slot, k], peer,
                 ).wait_recv()
         for j in range(8):
@@ -271,7 +285,7 @@
             rows = slice(OWNED * j, OWNED * (j + 1))
             row_rows = slice(OWNED * (j % 4), OWNED * (j % 4 + 1))
             copy = push(
-                send_buf.at[slot, part(h)], col_buf.at[slot, part(h), rows],
+                new_p.at[part(h)], col_buf.at[slot, part(h), rows],
                 own_s.at[slot, 0, h], col_r.at[slot, j, h], x_peers[0],
             )
             arrives = jnp.logical_or(
@@ -287,7 +301,9 @@
                 col_buf[slot, part(h), rows, :] = row_buf[slot, part(h), row_rows, :]
 
     pl.semaphore_wait(barrier, 30)
-    gather_start(0)
+    cross(0)
+    spread(0, send_buf.at[0])
+    spread_row(0, send_buf.at[0])
     fit_start(0, gain, dual)
 
     flux_copy.wait()
@@ -302,27 +318,32 @@
         == lax.broadcasted_iota(jnp.int32, (8, LANES), 1) // 16
     ).astype(F32)
     col_block = pl.ds(pl.multiple_of(x * LANES, LANES), LANES)
+    far_block = pl.ds(pl.multiple_of(far_col * LANES, LANES), LANES)
     samples = jnp.zeros((4, 1), F32)
     flags_copy.wait()
     for fp in range(PAIRS):
-        for place, table in ((col_block, flag_col), (block, flag_row)):
+        for place, table in ((col_block, flag_col), (block, flag_row), (far_block, None)):
             live = jnp.concatenate(
                 [flags_ref[2 * fp, :, place], flags_ref[2 * fp + 1, :, place]], axis=0
             ).astype(F32)
-            table[fp] = lax.dot_general(
+            table = flag_tmp if table is None else table.at[fp]
+            table[...] = lax.dot_general(
                 live, pair_hot, (((0,), (0,)), ((), ())), preferred_element_type=F32
             )
+        flag_far[fp] = flag_tmp[pl.ds(own_at, OWNED), :]
         for f in (2 * fp, 2 * fp + 1):
             count = jnp.sum(flags_ref[f].astype(F32), axis=1, keepdims=True)
             samples = samples + count * (count - 1.0)
     samples = jnp.sum(samples, axis=0, keepdims=True)
 
     rmat[...] = jnp.zeros_like(rmat)
-    gather_relay(0)
+    for h in range(CHUNKS):
+        across(0, h).wait_recv()
+        relay(0, relay_buf.at[0], h)
     smooth = fit_finish(0)
     for i in range(PAIRS):
         send_buf[1, i] = turned(smooth[i] - dual[i], i)
-    gather_start(1)
+    cross(1)
 
     vis_copy.wait()
     row_id = row * 64 + lax.broadcasted_iota(jnp.int32, (64, LANES), 0)
@@ -346,11 +367,8 @@
 
     def arrange(it, fp):
         flux = flux_tab[pl.ds(fp, 1), :]
-        b = col_buf[0, fp]
-        p = row_buf[0, fp]
-        if it > 0:
-            b = b + col_buf[1, fp] * col_buf[2, fp]
-            p = p + row_buf[1, fp] * row_buf[2, fp]
+        b = col_buf[it, fp]
+        p = row_buf[it, fp]
         b = b * flux
         t_buf[it, pl.ds(fp, 1), :] = jnp.sum(b * b * flag_col[fp], axis=0, keepdims=True)
         turned_b = b.T
@@ -370,6 +388,37 @@
                 rmat[f, t, 16 * t : 16 * t + 16, :] = high
                 rmat[f, t, 64 + 16 * t : 64 + 16 * t + 16, :] = rest
 
+    def numerators(it, first, end):
+        def pair(fp, carry):
+            halves = []
+            for f2 in range(2):
+                f = 2 * fp + f2
+                total = jnp.zeros((LANES, LANES), F32)
+                for t in range(4):
+                    high, rest = split(resid[f, t])
+                    total = total + lax.dot_general(
+                        jnp.concatenate([high, rest], axis=0), rmat[f, t],
+                        (((1,), (1,)), ((), ())), preferred_element_type=F32,
+                    )
+                halves.append(both(total[0:64] + total[64:128]))
+            num_buf[it, fp] = jnp.where(low, halves[0], halves[1])
+            return carry
+
+        lax.fori_loop(first, end, pair, 0, unroll=True)
+
+    def exchange(it, k, peer, there, h):
+        rows = pl.ds(pl.multiple_of(there * OWNED, OWNED), OWNED)
+        return push(
+            num_buf.at[it, part(h), rows], num_recv.at[it, k, part(h)],
+            num_s.at[it, k, h], num_r.at[it, k, h], peer,
+        )
+
+    def exchange_start(it, h):
+        for k, peer in enumerate(x_peers):
+            copy = exchange(it, k, peer, lax.rem(x + k + 1, 4), h)
+            copy.start()
+            pending.append(copy)
+
     def products(it):
         def residual(f, squares):
             for t in range(4):
@@ -377,46 +426,28 @@
                 model = model[0:64] + model[64:128]
                 w = weight[f, t]
                 r = wvis[f, t] - jnp.concatenate([w, w], axis=1) * model
-                high, rest = split(r)
-                rhi[f, t, 0:64, :] = high
-                rhi[f, t, 64:128, :] = rest
+                resid[f, t] = r
                 squares = squares + jnp.sum((r * r).reshape(8, 8, 2 * LANES), axis=0)
             return squares
 
         squares = jnp.zeros((8, 2 * LANES), F32)
         for h in range(CHUNKS):
-            gather_finish(2 * it, h)
+            gather_finish(it, h)
             first, end = h * PAIRS // CHUNKS, (h + 1) * PAIRS // CHUNKS
 
             def arranged(fp, carry):
                 arrange(it, fp)
                 return carry
 
-            lax.fori_loop(first, end, arranged, 0)
-            squares = lax.fori_loop(2 * first, 2 * end, residual, squares)
+            lax.fori_loop(first, end, arranged, 0, unroll=True)
+            squares = lax.fori_loop(2 * first, 2 * end, residual, squares, unroll=True)
         squares = squares[:, 0:LANES] + squares[:, LANES:]
         return jnp.sum(squares, axis=0, keepdims=True)
 
-    def numerators(it):
-        def pair(fp, carry):
-            halves = []
-            for f2 in range(2):
-                f = 2 * fp + f2
-                total = jnp.zeros((LANES, LANES), F32)
-                for t in range(4):
-                    total = total + lax.dot_general(
-                        rhi[f, t], rmat[f, t], (((1,), (1,)), ((), ())),
-                        preferred_element_type=F32,
-                    )
-                halves.append(both(total[0:64] + total[64:128]))
-            num_buf[it, fp] = jnp.where(low, halves[0], halves[1])
-            return carry
-
-        lax.fori_loop(0, PAIRS, pair, 0)
-
-    def squares_start(it, stage, value, peers):
+    def squares_start(it, stage, value, peers, order):
         sq_send[it, stage] = value
-        for k, peer in enumerate(peers):
+        for k in order:
+            peer = peers[k]
             copy = push(
                 sq_send.at[it, stage], sq_recv.at[it, stage, k],
                 sq_s.at[it, stage, k], sq_r.at[it, stage, k], peer,
@@ -435,23 +466,10 @@
             total = total + sq_recv[it, stage, k]
         return total
 
-    def exchange_start(it):
-        for k, peer in enumerate(x_peers):
-            there = lax.rem(x + k + 1, 4)
-            rows = pl.ds(pl.multiple_of(there * OWNED, OWNED), OWNED)
-            copy = push(
-                num_buf.at[it, :, rows], num_recv.at[it, k],
-                num_s.at[it, k], num_r.at[it, k], peer,
-            )
-            copy.start()
-            pending.append(copy)
-
     def exchange_finish(it):
         for k, peer in enumerate(x_peers):
-            push(
-                num_buf.at[it, :, x_rows], num_recv.at[it, k],
-                num_s.at[it, k], num_r.at[it, k], peer,
-            ).wait_recv()
+            for h in range(CHUNKS):
+                exchange(it, k, peer, x, h).wait_recv()
             push(t_buf.at[it], t_recv.at[it, k], t_s.at[it, k], t_r.at[it, k], peer).wait_recv()
         num = num_buf[it, :, x_rows, :]
         power = t_buf[it]
@@ -468,30 +486,28 @@
 
     for it in range(ITERS):
         squares = products(it)
-        squares_start(it, 0, squares, plane_peers)
+        squares_start(it, 0, squares, plane_peers, plane_order)
         for k, peer in enumerate(x_peers):
             copy = push(t_buf.at[it], t_recv.at[it, k], t_s.at[it, k], t_r.at[it, k], peer)
             copy.start()
             pending.append(copy)
-        numerators(it)
-        exchange_start(it)
-        if it == 0:
-            gather_relay(1)
-            num, power = exchange_finish(it)
-            send_buf[2] = num
-            gather_start(2)
+        for h in range(CHUNKS):
+            numerators(it, h * PAIRS // CHUNKS, (h + 1) * PAIRS // CHUNKS)
+            exchange_start(it, h)
         squares = squares_finish(it, 0, plane_peers)
         squares = jnp.sum(squares, axis=1, keepdims=True)
         squares_start(
             it, 1,
-            jnp.where(lane == 0, squares, jnp.where(lane == 1, samples, 0.0)), line_peers,
-        )
-        if it == 0:
-            gather_relay(2)
-        else:
+            jnp.where(lane == 0, squares, jnp.where(lane == 1, samples, 0.0)),
+            line_peers, line_order,
+        )
+        if it > 0:
             smooth = fit_finish(it)
             dual = [dual[i] + gain[i] - smooth[i] for i in range(PAIRS)]
-            num, power = exchange_finish(it)
+        num, power = exchange_finish(it)
+        if it + 1 < ITERS:
+            send_buf[2] = num
+            cross(2)
         parts = []
         for i in range(PAIRS):
             target = smooth[i] - dual[i]
@@ -501,6 +517,13 @@
             )
             numer = num[i] * cos[i] - swapped(num[i]) * sin[i]
             parts.append((numer + den * gain[i], den, target))
+        if it + 1 < ITERS:
+            crossed(1)
+            far = []
+            for i in range(PAIRS):
+                p = relay_buf[0, i]
+                den = solve_for(p, flag_far[i], flux_tab[i : i + 1, :], power[i : i + 1])
+                far.append((p, den, relay_buf[1, i]))
         total = squares_finish(it, 1, line_peers)
         count = 0.5 * jnp.sum(jnp.where(lane == 1, total, 0.0), axis=1, keepdims=True)
         total = jnp.sum(jnp.where(lane == 0, total, 0.0), axis=1, keepdims=True)
@@ -509,28 +532,26 @@
             0.5 * (gain[i] + (top + rho * target) / (den + rho))
             for i, (top, den, target) in enumerate(parts)
         ]
+        if it + 1 < ITERS:
+            for i in range(PAIRS):
+                new_p[i] = turned(gain[i], i)
+            spread(it + 1, new_p)
+            crossed(2)
+            for i, (p, den, turn) in enumerate(far):
+                far_p[i] = 0.5 * (
+                    p + (relay_buf[2, i] + den * p + rho * turn) / (den + rho)
+                )
+            for h in range(CHUNKS):
+                relay(it + 1, far_p, h)
+            spread_row(it + 1, new_p)
         fit_start(it + 1, gain, dual)
-        if it + 1 < ITERS:
-            for h in range(CHUNKS):
-                gather_finish(1, h)
-            for i in range(PAIRS):
-                flux, every = flux_tab[i : i + 1, :], power[i : i + 1]
-                for buf, live in (
-                    (row_buf, flag_row[i, pl.ds(row_half, 64), :]),
-                    (col_buf, flag_col[i]),
-                ):
-                    p = buf[0, i]
-                    den = solve_for(p, live, flux, every)
-                    share = 0.5 / (den + rho)
-                    buf[0, i] = 0.5 * p + share * (den * p + rho * buf[1, i])
-                    buf[1, i] = share
 
     for i in range(PAIRS):
-        gains_out[2 * i : 2 * i + 2] = gain[i].T.reshape(2, 4, 2, 8, OWNED)
+        solved[0, i] = gain[i]
     smooth = fit_finish(ITERS)
     for i in range(PAIRS):
         value = dual[i] + gain[i] - smooth[i]
-        duals_out[2 * i : 2 * i + 2] = value.T.reshape(2, 4, 2, 8, OWNED)
+        solved[1, i] = value
 
     for copy in pending:
         copy.wait_send()
@@ -539,22 +560,25 @@
     def _():
         for slot in range(GATHERS):
             for h in range(CHUNKS):
-                to_far_col(slot, h).wait_send()
+                to_far_col(slot, far_p, h).wait_send()
+
+
+def placed(solved, gains_out, duals_out):
+    for k, out in enumerate((gains_out, duals_out)):
+        for i in range(PAIRS):
+            out[2 * i : 2 * i + 2] = solved[k, i].T.reshape(2, 4, 2, 8, OWNED)
 
 
 def shards(vis, flags, positions, lmn, flux, gains, duals):
     vmem = pl.BlockSpec(memory_space=pltpu.VMEM)
     positions = jnp.swapaxes(positions, 0, 1)
     dma = pltpu.SemaphoreType.DMA
-    return pl.pallas_call(
+    solved = pl.pallas_call(
         kernel,
         name="admm",
-        out_shape=(
-            jax.ShapeDtypeStruct(gains.shape, F32),
-            jax.ShapeDtypeStruct(duals.shape, F32),
-        ),
+        out_shape=jax.ShapeDtypeStruct((2, PAIRS, OWNED, LANES), F32),
         in_specs=[pl.BlockSpec(memory_space=pltpu.HBM)] * 7,
-        out_specs=(vmem, vmem),
+        out_specs=vmem,
         scratch_shapes=[
             pltpu.VMEM(vis.shape, BF16),
             pltpu.VMEM(flags.shape, jnp.int32),
@@ -567,11 +591,11 @@
             pltpu.VMEM((8, 4, 64, LANES), F32),
             pltpu.VMEM((8, 4, LANES, 2 * LANES), BF16),
             pltpu.VMEM((8, LANES, LANES), BF16),
-            pltpu.VMEM((8, 4, LANES, 2 * LANES), BF16),
+            pltpu.VMEM((8, 4, 64, 2 * LANES), F32),
             pltpu.VMEM((GATHERS, PAIRS, 64, LANES), F32),
             pltpu.VMEM((GATHERS, PAIRS, LANES, LANES), F32),
-            pltpu.VMEM((GATHERS, PAIRS, OWNED, LANES), F32),
-            pltpu.VMEM((GATHERS, PAIRS, OWNED, LANES), F32),
+            pltpu.VMEM((CROSSED, PAIRS, OWNED, LANES), F32),
+            pltpu.VMEM((CROSSED, PAIRS, OWNED, LANES), F32),
             pltpu.VMEM((ITERS, PAIRS, 64, LANES), F32),
             pltpu.VMEM((ITERS, 3, PAIRS, OWNED, LANES), F32),
             pltpu.VMEM((ITERS, PAIRS, LANES), F32),
@@ -583,13 +607,17 @@
             pltpu.VMEM((PAIRS, LANES, LANES), F32),
             pltpu.VMEM((PAIRS, LANES, LANES), F32),
             pltpu.VMEM((LANES, LANES), F32),
+            pltpu.VMEM((PAIRS, OWNED, LANES), F32),
+            pltpu.VMEM((PAIRS, OWNED, LANES), F32),
+            pltpu.VMEM((PAIRS, OWNED, LANES), F32),
+            pltpu.VMEM((LANES, LANES), F32),
             pltpu.VMEM((PAIRS, LANES), F32),
             dma((7,)),
             dma((GATHERS, 3)), dma((GATHERS, 3)),
-            dma((GATHERS, CHUNKS)), dma((GATHERS, CHUNKS)),
+            dma((CROSSED, CHUNKS)), dma((CROSSED, CHUNKS)),
             dma((GATHERS, 4, CHUNKS)), dma((GATHERS, 4, CHUNKS)),
             dma((GATHERS, 8, CHUNKS)),
-            dma((ITERS, 3)), dma((ITERS, 3)),
+            dma((ITERS, 3, CHUNKS)), dma((ITERS, 3, CHUNKS)),
             dma((ITERS, 3)), dma((ITERS, 3)),
             dma((ITERS, 2, 15)), dma((ITERS, 2, 15)),
             dma((ITERS + 1, 7)), dma((ITERS + 1, 7)),
@@ -598,6 +626,16 @@
             collective_id=0, has_side_effects=True, vmem_limit_bytes=60 * 1024 * 1024
         ),
     )(vis, flags, positions, lmn, flux, gains, duals)
+    return pl.pallas_call(
+        placed,
+        name="placed",
+        out_shape=(
+            jax.ShapeDtypeStruct(gains.shape, F32),
+            jax.ShapeDtypeStruct(duals.shape, F32),
+        ),
+        in_specs=[vmem],
+        out_specs=(vmem, vmem),
+    )(solved)
 
 
 def solution(mesh):

time: 64.9 us -> 61.4 us (0.946)
  local copies, waits for them, and re-layouts: 2.42 us -> 0 us
  Pallas kernels: 61.7 us -> 60.6 us
    unnamed x4 -> x0, local copies, waits for them, and re-layouts: 2.42 us -> none
    pallas_call x1 -> x2, Pallas kernels: 61.7 us -> 60.6 us  [the longest x1 58.8 us: shards(): pl.pallas_call(kernel, name='admm', out_shape=jax.ShapeDtypeStruct((2, PA...]
where the time goes in v3:
time: 61.4 us; the launch traced here: 61.2 us
  Pallas kernels  60.6 us (99%)
  between operations  0.64 us (1%)
    pallas_call x1, Pallas kernels, shards(): pl.pallas_call(kernel, name='admm', out_shape=jax.ShapeDtypeStruct((2, PA...  58.8 us
    pallas_call x1, Pallas kernels, shards(): pl.pallas_call(placed, name='placed', out_shape=(jax.ShapeDtypeStruct(gai...  1.77 us

profile of v3, /device:TPU:1, one launch (start us, length us, event | category | flops | bytes accessed | tf_op | source)
XLA Modules:
  0.0 61.2 jit_solution(1611419706948350500)
XLA Ops:
  0.6 58.8 %admm.1.solved = f32[2,4,16,128]{3,2,1,0:T(8,128)} custom-call(bf16[8,4,2,64,128]{4,3,2,1,0:T(8,128)(2,1)} %vis_hbm.1, s32[8,4,512]{2,1,0:T(4,128)} %flags_hbm.1, f32[3,4,512]{2,1,0:T(4,128)} %bitcast.1, f32[3,8]{1,0:T(4,128)} %lmn_hbm.1, f32[8,8]{1,0:T(8,128)} %flux_hbm.1, f32[8,4,2,8,16]{4,3,2,1,0:T(8,128)} %gains_hbm.1, f32[8,4,2,8,16]{4,3,2,1,0:T(8,128)} %duals_hbm.1), custom_call_target="tpu_custom_call" | custom-call | tf_op jit(solution)/shard_map/admm/pallas_call | solution.py:576
  59.5 1.8 %placed.1 = (f32[8,4,2,8,16]{4,3,2,1,0:T(8,128)}, f32[8,4,2,8,16]{4,3,2,1,0:T(8,128)}) custom-call(f32[2,4,16,128]{3,2,1,0:T(8,128)} %admm.1.solved), custom_call_target="tpu_custom_call" | custom-call | tf_op jit(solution)/shard_map/placed/pallas_call | solution.py:629

commit v4 on v3

--- a/solution.py
+++ b/solution.py
@@ -44,11 +44,11 @@
 
 def kernel(
     vis_hbm, flags_hbm, pos_hbm, lmn_hbm, flux_hbm, gains_hbm, duals_hbm,
-    solved,
+    solved_hbm,
     vis_buf, flags_ref, pos_ref, lmn_ref, flux_ref, gains_ref, duals_ref, wvis, weight, rmat, lhs, resid,
     row_buf, col_buf, relay_buf, send_buf, num_buf, num_recv,
     t_buf, t_recv, fit_send, fit_recv, sq_send, sq_recv,
-    flag_col, flag_row, flag_tmp, flag_far, new_p, far_p, geom_blk, flux_tab,
+    flag_col, flag_row, flag_tmp, flag_far, new_p, far_p, geom_blk, flux_tab, solved,
     in_sem, row_s, row_r, rel_s, rel_r, own_s, fwd_s, col_r,
     num_s, num_r, t_s, t_r, sq_s, sq_r, fit_s, fit_r,
 ):
@@ -83,6 +83,11 @@
         )
 
     pending = []
+
+    def drain(count):
+        for copy in pending[:count]:
+            copy.wait_send()
+        del pending[:count]
 
     gains_copy, pos_copy, lmn_copy, flux_copy, duals_copy, flags_copy, vis_copy = (
         pltpu.make_async_copy(src, dst, in_sem.at[i])
@@ -228,14 +233,13 @@
             across(slot, h).wait_recv()
 
     def spread(slot, src):
-        copies = []
-        for h in range(CHUNKS):
-            for k in (2, 1, 3):
-                copies.append(push(
-                    src.at[part(h)], col_buf.at[slot, part(h), slot_rows],
-                    own_s.at[slot, k, h], col_r.at[slot, own_slot, h],
-                    at(y=lax.rem(y + k, 4), x=own_col),
-                ))
+        copies = [
+            push(
+                src, col_buf.at[slot, :, slot_rows], own_s.at[slot, k],
+                col_r.at[slot, own_slot, 0], at(y=lax.rem(y + k, 4), x=own_col),
+            )
+            for k in (2, 1, 3)
+        ]
         for copy in copies:
             copy.start()
         pending.extend(copies)
@@ -284,21 +288,30 @@
             from_y = lax.rem(x, 2) * 2 + j // 4
             rows = slice(OWNED * j, OWNED * (j + 1))
             row_rows = slice(OWNED * (j % 4), OWNED * (j % 4 + 1))
-            copy = push(
+            elsewhere = jnp.logical_or(from_y != y, x != j % 4)
+            piece = push(
                 new_p.at[part(h)], col_buf.at[slot, part(h), rows],
-                own_s.at[slot, 0, h], col_r.at[slot, j, h], x_peers[0],
-            )
-            arrives = jnp.logical_or(
-                from_y != y, jnp.logical_and(jnp.logical_not(near), x != j % 4)
-            )
-
-            @pl.when(arrives)
-            def _(copy=copy):
-                copy.wait_recv()
-
-            @pl.when(jnp.logical_and(from_y == y, near))
+                own_s.at[slot, 0], col_r.at[slot, j, h], x_peers[0],
+            )
+
+            @pl.when(jnp.logical_and(jnp.logical_not(near), elsewhere))
+            def _(piece=piece):
+                piece.wait_recv()
+
+            if h > 0:
+                continue
+            block = push(
+                new_p, col_buf.at[slot, :, rows],
+                own_s.at[slot, 0], col_r.at[slot, j, 0], x_peers[0],
+            )
+
+            @pl.when(jnp.logical_and(near, from_y != y))
+            def _(block=block):
+                block.wait_recv()
+
+            @pl.when(jnp.logical_and(near, from_y == y))
             def _(rows=rows, row_rows=row_rows):
-                col_buf[slot, part(h), rows, :] = row_buf[slot, part(h), row_rows, :]
+                col_buf[slot, :, rows, :] = row_buf[slot, :, row_rows, :]
 
     pl.semaphore_wait(barrier, 30)
     cross(0)
@@ -406,16 +419,16 @@
 
         lax.fori_loop(first, end, pair, 0, unroll=True)
 
-    def exchange(it, k, peer, there, h):
+    def exchange(it, k, peer, there):
         rows = pl.ds(pl.multiple_of(there * OWNED, OWNED), OWNED)
         return push(
-            num_buf.at[it, part(h), rows], num_recv.at[it, k, part(h)],
-            num_s.at[it, k, h], num_r.at[it, k, h], peer,
-        )
-
-    def exchange_start(it, h):
+            num_buf.at[it, :, rows], num_recv.at[it, k],
+            num_s.at[it, k], num_r.at[it, k], peer,
+        )
+
+    def exchange_start(it):
         for k, peer in enumerate(x_peers):
-            copy = exchange(it, k, peer, lax.rem(x + k + 1, 4), h)
+            copy = exchange(it, k, peer, lax.rem(x + k + 1, 4))
             copy.start()
             pending.append(copy)
 
@@ -468,8 +481,7 @@
 
     def exchange_finish(it):
         for k, peer in enumerate(x_peers):
-            for h in range(CHUNKS):
-                exchange(it, k, peer, x, h).wait_recv()
+            exchange(it, k, peer, x).wait_recv()
             push(t_buf.at[it], t_recv.at[it, k], t_s.at[it, k], t_r.at[it, k], peer).wait_recv()
         num = num_buf[it, :, x_rows, :]
         power = t_buf[it]
@@ -491,11 +503,11 @@
             copy = push(t_buf.at[it], t_recv.at[it, k], t_s.at[it, k], t_r.at[it, k], peer)
             copy.start()
             pending.append(copy)
-        for h in range(CHUNKS):
-            numerators(it, h * PAIRS // CHUNKS, (h + 1) * PAIRS // CHUNKS)
-            exchange_start(it, h)
+        numerators(it, 0, PAIRS)
+        exchange_start(it)
         squares = squares_finish(it, 0, plane_peers)
         squares = jnp.sum(squares, axis=1, keepdims=True)
+        started = len(pending)
         squares_start(
             it, 1,
             jnp.where(lane == 0, squares, jnp.where(lane == 1, samples, 0.0)),
@@ -524,6 +536,7 @@
                 p = relay_buf[0, i]
                 den = solve_for(p, flag_far[i], flux_tab[i : i + 1, :], power[i : i + 1])
                 far.append((p, den, relay_buf[1, i]))
+        drain(started)
         total = squares_finish(it, 1, line_peers)
         count = 0.5 * jnp.sum(jnp.where(lane == 1, total, 0.0), axis=1, keepdims=True)
         total = jnp.sum(jnp.where(lane == 0, total, 0.0), axis=1, keepdims=True)
@@ -544,17 +557,14 @@
             for h in range(CHUNKS):
                 relay(it + 1, far_p, h)
             spread_row(it + 1, new_p)
+        started = len(pending)
         fit_start(it + 1, gain, dual)
 
     for i in range(PAIRS):
         solved[0, i] = gain[i]
-    smooth = fit_finish(ITERS)
-    for i in range(PAIRS):
-        value = dual[i] + gain[i] - smooth[i]
-        solved[1, i] = value
-
-    for copy in pending:
-        copy.wait_send()
+    keep_gain = pltpu.make_async_copy(solved.at[0], solved_hbm.at[0], in_sem.at[7])
+    keep_gain.start()
+    drain(started)
 
     @pl.when(x != far_col)
     def _():
@@ -562,15 +572,37 @@
             for h in range(CHUNKS):
                 to_far_col(slot, far_p, h).wait_send()
 
-
-def placed(solved, gains_out, duals_out):
+    smooth = fit_finish(ITERS)
+    for i in range(PAIRS):
+        value = dual[i] + gain[i] - smooth[i]
+        solved[1, i] = value
+    keep_dual = pltpu.make_async_copy(solved.at[1], solved_hbm.at[1], in_sem.at[8])
+    keep_dual.start()
+
+    drain(len(pending))
+    keep_gain.wait()
+    keep_dual.wait()
+
+
+def placed(solved, gains_out, duals_out, dense, laid, in_sem, out_sem):
+    loads = [
+        pltpu.make_async_copy(solved.at[k], dense.at[k], in_sem.at[k]) for k in range(2)
+    ]
+    for load in loads:
+        load.start()
+    stores = []
     for k, out in enumerate((gains_out, duals_out)):
+        loads[k].wait()
         for i in range(PAIRS):
-            out[2 * i : 2 * i + 2] = solved[k, i].T.reshape(2, 4, 2, 8, OWNED)
+            laid[k, 2 * i : 2 * i + 2] = dense[k, i].T.reshape(2, 4, 2, 8, OWNED)
+        stores.append(pltpu.make_async_copy(laid.at[k], out, out_sem.at[k]))
+        stores[k].start()
+    for store in stores:
+        store.wait()
 
 
 def shards(vis, flags, positions, lmn, flux, gains, duals):
-    vmem = pl.BlockSpec(memory_space=pltpu.VMEM)
+    hbm = pl.BlockSpec(memory_space=pltpu.HBM)
     positions = jnp.swapaxes(positions, 0, 1)
     dma = pltpu.SemaphoreType.DMA
     solved = pl.pallas_call(
@@ -578,7 +610,7 @@
         name="admm",
         out_shape=jax.ShapeDtypeStruct((2, PAIRS, OWNED, LANES), F32),
         in_specs=[pl.BlockSpec(memory_space=pltpu.HBM)] * 7,
-        out_specs=vmem,
+        out_specs=hbm,
         scratch_shapes=[
             pltpu.VMEM(vis.shape, BF16),
             pltpu.VMEM(flags.shape, jnp.int32),
@@ -612,12 +644,13 @@
             pltpu.VMEM((PAIRS, OWNED, LANES), F32),
             pltpu.VMEM((LANES, LANES), F32),
             pltpu.VMEM((PAIRS, LANES), F32),
-            dma((7,)),
+            pltpu.VMEM((2, PAIRS, OWNED, LANES), F32),
+            dma((9,)),
             dma((GATHERS, 3)), dma((GATHERS, 3)),
             dma((CROSSED, CHUNKS)), dma((CROSSED, CHUNKS)),
-            dma((GATHERS, 4, CHUNKS)), dma((GATHERS, 4, CHUNKS)),
+            dma((GATHERS, 4)), dma((GATHERS, 4, CHUNKS)),
             dma((GATHERS, 8, CHUNKS)),
-            dma((ITERS, 3, CHUNKS)), dma((ITERS, 3, CHUNKS)),
+            dma((ITERS, 3)), dma((ITERS, 3)),
             dma((ITERS, 3)), dma((ITERS, 3)),
             dma((ITERS, 2, 15)), dma((ITERS, 2, 15)),
             dma((ITERS + 1, 7)), dma((ITERS + 1, 7)),
@@ -633,8 +666,13 @@
             jax.ShapeDtypeStruct(gains.shape, F32),
             jax.ShapeDtypeStruct(duals.shape, F32),
         ),
-        in_specs=[vmem],
-        out_specs=(vmem, vmem),
+        in_specs=[hbm],
+        out_specs=(hbm, hbm),
+        scratch_shapes=[
+            pltpu.VMEM((2, PAIRS, OWNED, LANES), F32),
+            pltpu.VMEM((2, *gains.shape), F32),
+            dma((2,)), dma((2,)),
+        ],
     )(solved)
 
 

time: 61.4 us -> 61.2 us (level)
  no operation moved by 1% of the time
where the time goes in v4:
time: 61.2 us; the launch traced here: 61.1 us
  Pallas kernels  60.4 us (99%)
  between operations  0.64 us (1%)
    pallas_call x1, Pallas kernels, shards(): pl.pallas_call(kernel, name='admm', out_shape=jax.ShapeDtypeStruct((2, PA...  58.7 us
    pallas_call x1, Pallas kernels, shards(): pl.pallas_call(placed, name='placed', out_shape=(jax.ShapeDtypeStruct(gai...  1.76 us

profile of v4, /device:TPU:1, one launch (start us, length us, event | category | flops | bytes accessed | tf_op | source)
XLA Modules:
  0.0 61.1 jit_solution(5503346053243259581)
XLA Ops:
  0.6 58.7 %admm.1.solved = f32[2,4,16,128]{3,2,1,0:T(8,128)} custom-call(bf16[8,4,2,64,128]{4,3,2,1,0:T(8,128)(2,1)} %vis_hbm.1, s32[8,4,512]{2,1,0:T(4,128)} %flags_hbm.1, f32[3,4,512]{2,1,0:T(4,128)} %bitcast.1, f32[3,8]{1,0:T(4,128)} %lmn_hbm.1, f32[8,8]{1,0:T(8,128)} %flux_hbm.1, f32[8,4,2,8,16]{4,3,2,1,0:T(8,128)} %gains_hbm.1, f32[8,4,2,8,16]{4,3,2,1,0:T(8,128)} %duals_hbm.1), custom_call_target="tpu_custom_call" | custom-call | tf_op jit(solution)/shard_map/admm/pallas_call | solution.py:608
  59.3 1.8 %placed.1 = (f32[8,4,2,8,16]{4,3,2,1,0:T(8,128)}, f32[8,4,2,8,16]{4,3,2,1,0:T(8,128)}) custom-call(f32[2,4,16,128]{3,2,1,0:T(8,128)} %admm.1.solved), custom_call_target="tpu_custom_call" | custom-call | tf_op jit(solution)/shard_map/placed/pallas_call | solution.py:662

commit v5 on v4

--- a/solution.py
+++ b/solution.py
@@ -392,7 +392,9 @@
             for start, value in ((0, p_high), (64, p_low)):
                 other = pltpu.roll(value, 64, 1)
                 pieces = (value, other) if f2 == 0 else (other, value)
-                lhs[f, start : start + 64, :] = jnp.where(low, *pieces).astype(BF16)
+                if start > 0:
+                    pieces = (pieces[0], 0.0)
+                lhs[f, :, 2 * start : 2 * start + LANES] = jnp.where(low, *pieces).astype(BF16)
             for t in range(4):
                 start = 64 * f2 + 16 * t
                 left = turned_b[start : start + 16]
@@ -400,6 +402,7 @@
                 high, rest = split(jnp.concatenate([left, right], axis=1))
                 rmat[f, t, 16 * t : 16 * t + 16, :] = high
                 rmat[f, t, 64 + 16 * t : 64 + 16 * t + 16, :] = rest
+                rmat[f, t, 128 + 16 * t : 128 + 16 * t + 16, :] = high
 
     def numerators(it, first, end):
         def pair(fp, carry):
@@ -410,7 +413,7 @@
                 for t in range(4):
                     high, rest = split(resid[f, t])
                     total = total + lax.dot_general(
-                        jnp.concatenate([high, rest], axis=0), rmat[f, t],
+                        jnp.concatenate([high, rest], axis=0), rmat[f, t, 0:LANES, :],
                         (((1,), (1,)), ((), ())), preferred_element_type=F32,
                     )
                 halves.append(both(total[0:64] + total[64:128]))
@@ -436,7 +439,6 @@
         def residual(f, squares):
             for t in range(4):
                 model = jnp.dot(lhs[f], rmat[f, t], preferred_element_type=F32)
-                model = model[0:64] + model[64:128]
                 w = weight[f, t]
                 r = wvis[f, t] - jnp.concatenate([w, w], axis=1) * model
                 resid[f, t] = r
@@ -621,8 +623,8 @@
             pltpu.VMEM(duals.shape, F32),
             pltpu.VMEM((8, 4, 64, 2 * LANES), F32),
             pltpu.VMEM((8, 4, 64, LANES), F32),
-            pltpu.VMEM((8, 4, LANES, 2 * LANES), BF16),
-            pltpu.VMEM((8, LANES, LANES), BF16),
+            pltpu.VMEM((8, 4, 2 * LANES, 2 * LANES), BF16),
+            pltpu.VMEM((8, 64, 2 * LANES), BF16),
             pltpu.VMEM((8, 4, 64, 2 * LANES), F32),
             pltpu.VMEM((GATHERS, PAIRS, 64, LANES), F32),
             pltpu.VMEM((GATHERS, PAIRS, LANES, LANES), F32),

time: 61.2 us -> 61.5 us (level)
  no operation moved by 1% of the time
where the time goes in v5:
time: 61.5 us; the launch traced here: 61.3 us
  Pallas kernels  60.7 us (99%)
  between operations  0.64 us (1%)
    pallas_call x1, Pallas kernels, shards(): pl.pallas_call(kernel, name='admm', out_shape=jax.ShapeDtypeStruct((2, PA...  58.9 us
    pallas_call x1, Pallas kernels, shards(): pl.pallas_call(placed, name='placed', out_shape=(jax.ShapeDtypeStruct(gai...  1.76 us

profile of v5, /device:TPU:1, one launch (start us, length us, event | category | flops | bytes accessed | tf_op | source)
XLA Modules:
  0.0 61.3 jit_solution(17717008967452147237)
XLA Ops:
  0.6 58.9 %admm.1.solved = f32[2,4,16,128]{3,2,1,0:T(8,128)} custom-call(bf16[8,4,2,64,128]{4,3,2,1,0:T(8,128)(2,1)} %vis_hbm.1, s32[8,4,512]{2,1,0:T(4,128)} %flags_hbm.1, f32[3,4,512]{2,1,0:T(4,128)} %bitcast.1, f32[3,8]{1,0:T(4,128)} %lmn_hbm.1, f32[8,8]{1,0:T(8,128)} %flux_hbm.1, f32[8,4,2,8,16]{4,3,2,1,0:T(8,128)} %gains_hbm.1, f32[8,4,2,8,16]{4,3,2,1,0:T(8,128)} %duals_hbm.1), custom_call_target="tpu_custom_call" | custom-call | tf_op jit(solution)/shard_map/admm/pallas_call | solution.py:610
  59.6 1.8 %placed.1 = (f32[8,4,2,8,16]{4,3,2,1,0:T(8,128)}, f32[8,4,2,8,16]{4,3,2,1,0:T(8,128)}) custom-call(f32[2,4,16,128]{3,2,1,0:T(8,128)} %admm.1.solved), custom_call_target="tpu_custom_call" | custom-call | tf_op jit(solution)/shard_map/placed/pallas_call | solution.py:664
